TPU v7x, 512 devices: a whole 4x4x16 slice. The times are simulated.
512 devices in a mesh: expert: 64 (over z, x), dp: 8 (over y, core).
Axes of the slice: x: 4, y: 4, z: 16, core: 2. Of those that a mesh axis runs over, the one named last changes fastest.
Arguments:
- tokens: bfloat16 [32768, 2048], P(('expert', 'dp')), may hold values from -6 to 6
- attn_partials: bfloat16 [8, 32768, 2048], P('dp', 'expert'), may hold values from -5 to 5
- expert_ids: int32 [32768], P(('expert', 'dp')), may hold values from 0 to 3, as said below
- gate: float32 [32768], P(('expert', 'dp')), may hold values from 0.2 to 1
- w_in: float32 [2048, 20480], P('dp', 'expert'), may hold values from -6 to 6
- w_out: float32 [2048, 20480], P('dp', 'expert'), may hold values from -6 to 6
Outputs:
- token_grad: bfloat16 [32768, 2048], P(('expert', 'dp'))
- new_w_in: float32 [2048, 20480], P('dp', 'expert')
- new_w_out: float32 [2048, 20480], P('dp', 'expert')
Inputs may be any that keep to these rules, and one draw needn't show every extreme that they name: `expert_ids`: one expert, the same for all devices, is chosen by half of the 64 rows of every device; the other experts share the remaining rows of a device as evenly as whole numbers allow.
All inputs are finite; a program needn't handle non-finite values.
Results may differ from a plain program's by a relative error of at most 0.025.
Values may be sent and summed in bfloat16 or wider, within the bound.
A program may use at most 64 MiB of HBM per device.

v0:
```python
import jax
import jax.numpy as jnp
from jax import lax
from jax.sharding import PartitionSpec as P

FF = 5120
SHARDS = 16


gelu_coef = 0.7978845608028654
cubic_coef = 0.044715
step_rate = 0.5


def gelu_value(inputs):
    return (
        0.5
        * inputs
        * (1.0 + jnp.tanh(gelu_coef * (inputs + cubic_coef * inputs * inputs * inputs)))
    )


def gelu_slope(inputs):
    tangent = jnp.tanh(gelu_coef * (inputs + cubic_coef * inputs * inputs * inputs))
    return 0.5 * (1.0 + tangent) + 0.5 * inputs * (1.0 - tangent * tangent) * gelu_coef * (
        1.0 + 3.0 * cubic_coef * inputs * inputs
    )


def contract_rows(left, right):
    return lax.dot_general(
        left, right, (((0,), (0,)), ((), ())), preferred_element_type=jnp.float32
    )


def contract_cols(left, right):
    return lax.dot_general(
        left, right, (((1,), (1,)), ((), ())), preferred_element_type=jnp.float32
    )


def summed_grads(attn_partials, gate):
    terms = attn_partials[0].astype(jnp.float32)
    out_grad = lax.psum_scatter(
        terms.astype(jnp.bfloat16), "dp", scatter_dimension=0, tiled=True
    ).astype(jnp.float32)
    return (gate[:, None] * out_grad).astype(jnp.bfloat16)


def shards(tokens, attn_partials, expert_ids, gate, w_in, w_out):
    tok_rows = tokens.shape[0]
    width = tokens.shape[1]
    n_expert = lax.axis_size("expert")
    experts = n_expert // SHARDS
    capacity = 5 * tok_rows // (8 * experts)
    scale_in = width ** (-0.5)
    scale_out = FF ** (-0.5)
    expert_range = jnp.arange(experts, dtype=jnp.int32)
    member = (expert_ids[:, None] == expert_range[None, :]).astype(jnp.int32)
    slot_rank = jnp.sum(member * (jnp.cumsum(member, axis=0) - 1), axis=1)
    keeping = slot_rank < capacity
    flat_slot = jnp.where(keeping, expert_ids * capacity + slot_rank, -1)
    slot_range = jnp.arange(experts * capacity, dtype=jnp.int32)
    dispatch = (slot_range[:, None] == flat_slot[None, :]).astype(jnp.bfloat16)

    def fan_out(source_rows):
        packed = jnp.dot(dispatch, source_rows, preferred_element_type=jnp.float32).astype(
            jnp.bfloat16
        )
        return jnp.repeat(packed.reshape(experts, capacity, width), SHARDS, axis=0)

    weights_in, weights_out = (
        lax.all_gather(w_in.astype(jnp.bfloat16), "dp", axis=0, tiled=True),
        lax.all_gather(w_out.astype(jnp.bfloat16), "dp", axis=0, tiled=True),
    )
    gated = summed_grads(attn_partials, gate)
    arrived, arrived_grads = (
        lax.all_to_all(fan_out(tokens), "expert", split_axis=0, concat_axis=0, tiled=True),
        lax.all_to_all(fan_out(gated), "expert", split_axis=0, concat_axis=0, tiled=True),
    )
    expert_rows = arrived.reshape(n_expert * capacity, width)
    grad_rows = arrived_grads.reshape(n_expert * capacity, width)
    pre_act = jnp.dot(expert_rows, weights_in, preferred_element_type=jnp.float32) * scale_in
    hidden = gelu_value(pre_act).astype(jnp.bfloat16)
    hidden_grad = jnp.dot(grad_rows, weights_out, preferred_element_type=jnp.float32) * scale_out
    pre_grad = (hidden_grad * gelu_slope(pre_act)).astype(jnp.bfloat16)
    partial_x = (contract_cols(pre_grad, weights_in) * scale_in).astype(jnp.bfloat16)
    returned = lax.all_to_all(
        partial_x.reshape(n_expert, capacity, width),
        "expert",
        split_axis=0,
        concat_axis=0,
        tiled=True,
    )
    slot_sums = jnp.sum(
        returned.reshape(experts, SHARDS, capacity, width).astype(jnp.float32), axis=1
    )
    safe_slot = jnp.maximum(flat_slot, 0)
    picked_sums = jnp.take(slot_sums.reshape(experts * capacity, width), safe_slot, axis=0)
    token_grad = jnp.where(keeping[:, None], picked_sums, 0.0).astype(jnp.bfloat16)
    rows_part = expert_rows
    grad_in = lax.psum_scatter(
        (contract_rows(rows_part, pre_grad) * scale_in).astype(jnp.bfloat16),
        "dp",
        scatter_dimension=0,
        tiled=True,
    ).astype(jnp.float32)
    rows_part = grad_rows
    grad_out = lax.psum_scatter(
        (contract_rows(rows_part, hidden) * scale_out).astype(jnp.bfloat16),
        "dp",
        scatter_dimension=0,
        tiled=True,
    ).astype(jnp.float32)
    new_w_in = w_in - step_rate * grad_in
    new_w_out = w_out - step_rate * grad_out
    return (token_grad, new_w_in, new_w_out)


def solution(mesh):
    in_specs = (
        P(("expert", "dp"), None),
        P("dp", "expert", None),
        P(("expert", "dp")),
        P(("expert", "dp")),
        P("dp", "expert"),
        P("dp", "expert"),
    )
    out_specs = (P(("expert", "dp"), None), P("dp", "expert"), P("dp", "expert"))
    return jax.shard_map(shards, mesh=mesh, in_specs=in_specs, out_specs=out_specs, check_vma=False)
```

profile of v0, /device:TPU:1, one launch (start us, length us, event | category | flops | bytes accessed | tf_op | source)
XLA Modules:
  0.0 719.5 jit_solution(7332507688326082465)
XLA Ops:
  7.2 0.0 copy-start
  7.2 0.8 fusion.13
  8.0 0.1 reduce_window_sum.11
  8.0 0.8 select_reduce_fusion
  8.9 0.7 broadcast_compare_fusion
  9.6 0.0 copy-done
  9.6 0.2 convolution_convert_fusion
  9.7 0.1 reshape.47
  9.8 2.6 broadcast_in_dim.44
  12.4 0.0 copy-start.3
  12.4 19.5 %all-to-all-start.1 = ((bf16[64,10,2048]{2,1,0:T(8,128)(2,1)}), bf16[64,10,2048]{2,1,0:T(8,128)(2,1)}, u32[]{:S(2)}, u32[]{:S(2)}) async-start(bf16[64,10,2048]{2,1,0:T(8,128)(2,1)} %bitcast.17), calls=%async_computation.2 | async-start | bytes 8388608 | tf_op jit(solution)/shard_map/all_to_all | solution.py:78
  31.9 0.0 reduce-scatter.4.cloned.1.call-start
  31.9 0.7 reduce-scatter.4.cloned.1.call-update
  32.6 44.5 %reduce-scatter.4.cloned.1.call-done = bf16[64,2048]{1,0:T(8,128)(2,1)} async-done(((bf16[512,2048]{1,0:T(8,128)(2,1)}), bf16[64,2048]{1,0:T(8,128)(2,1)}) %reduce-scatter.4.cloned.1.call-update) | async-done | bytes 262160 | tf_op jit(solution)/shard_map/reduce_scatter | solution.py:44
  77.1 0.0 copy-done.3
  77.1 1.2 convolution_convert_fusion.1
  78.3 0.1 reshape.44
  78.4 137.2 %all-to-all-done.1 = bf16[64,10,2048]{2,1,0:T(8,128)(2,1)} async-done(((bf16[64,10,2048]{2,1,0:T(8,128)(2,1)}), bf16[64,10,2048]{2,1,0:T(8,128)(2,1)}, u32[]{:S(2)}, u32[]{:S(2)}) %all-to-all-start.1) | async-done | bytes 2621472 | tf_op jit(solution)/shard_map/all_to_all | solution.py:78
  215.6 2.6 broadcast_in_dim.43
  218.2 0.0 copy-start.1
  218.2 12.0 %all-to-all-start = ((bf16[64,10,2048]{2,1,0:T(8,128)(2,1)}), bf16[64,10,2048]{2,1,0:T(8,128)(2,1)}, u32[]{:S(2)}, u32[]{:S(2)}) async-start(bf16[64,10,2048]{2,1,0:T(8,128)(2,1)} %bitcast.16), calls=%async_computation.1 | async-start | bytes 8388608 | tf_op jit(solution)/shard_map/all_to_all | solution.py:79
  230.2 0.0 all-gather.5.cloned.1.call-start
  230.3 0.0 copy-done.1
  230.3 0.7 convert_element_type.60
  231.0 0.0 all-gather.5.cloned.1.call-update
  231.0 0.0 reduce-scatter.8.cloned.1.call-start
  231.0 4.1 reshape.49
  235.1 32.7 %all-gather.5.cloned.1.call-done = bf16[2048,320]{0,1:T(8,128)(2,1)} async-done(((bf16[256,320]{0,1:T(8,128)(2,1)}), bf16[2048,320]{0,1:T(8,128)(2,1)}) %all-gather.5.cloned.1.call-update) | async-done | bytes 1310736 | tf_op jit(solution)/shard_map/all_gather | solution.py:73
  267.8 3.4 fusion.21
  271.3 142.7 %all-to-all-done = bf16[64,10,2048]{2,1,0:T(8,128)(2,1)} async-done(((bf16[64,10,2048]{2,1,0:T(8,128)(2,1)}), bf16[64,10,2048]{2,1,0:T(8,128)(2,1)}, u32[]{:S(2)}, u32[]{:S(2)}) %all-to-all-start) | async-done | bytes 2621472 | tf_op jit(solution)/shard_map/all_to_all | solution.py:79
  413.9 5.5 reshape.46
  419.4 0.0 copy-start.2
  419.4 4.4 fusion.1
  423.8 0.0 reduce-scatter.8.cloned.1.call-update
  423.8 0.0 all-gather.3.cloned.1.call-start
  423.9 36.6 %reduce-scatter.8.cloned.1.call-done = bf16[256,320]{0,1:T(8,128)(2,1)} async-done(((bf16[2048,320]{0,1:T(8,128)(2,1)}), bf16[256,320]{0,1:T(8,128)(2,1)}) %reduce-scatter.8.cloned.1.call-update) | async-done | bytes 163856 | tf_op jit(solution)/shard_map/reduce_scatter | solution.py:109
  460.5 0.0 copy-done.2
  460.5 1.7 multiply_subtract_fusion
  462.2 0.0 all-gather.3.cloned.1.call-update
  462.2 33.9 %all-gather.3.cloned.1.call-done = bf16[2048,320]{0,1:T(8,128)(2,1)} async-done(((bf16[256,320]{0,1:T(8,128)(2,1)}), bf16[2048,320]{0,1:T(8,128)(2,1)}) %all-gather.3.cloned.1.call-update) | async-done | bytes 1310736 | tf_op jit(solution)/shard_map/all_gather | solution.py:74
  496.2 0.0 copy-start.4
  496.2 4.0 fusion.3
  500.2 0.0 copy-start.5
  500.2 0.8 copy-done.5
  501.0 0.0 copy-done.4
  501.0 3.1 multiply_convert_fusion
  504.1 5.3 reshape.50
  509.4 15.5 %all-to-all-start.2 = ((bf16[64,10,2048]{2,1,0:T(8,128)(2,1)}), bf16[64,10,2048]{2,1,0:T(8,128)(2,1)}, u32[]{:S(2)}, u32[]{:S(2)}) async-start(bf16[64,10,2048]{2,1,0:T(8,128)(2,1)} %reshape.50), calls=%async_computation.3 | async-start | bytes 8388608 | tf_op jit(solution)/shard_map/all_to_all | solution.py:88
  524.9 0.0 reduce-scatter.6.cloned.1.call-start
  524.9 3.3 fusion
  528.2 0.0 reduce-scatter.6.cloned.1.call-update
  528.3 39.6 %reduce-scatter.6.cloned.1.call-done = bf16[256,320]{0,1:T(8,128)(2,1)} async-done(((bf16[2048,320]{0,1:T(8,128)(2,1)}), bf16[256,320]{0,1:T(8,128)(2,1)}) %reduce-scatter.6.cloned.1.call-update) | async-done | bytes 163856 | tf_op jit(solution)/shard_map/reduce_scatter | solution.py:102
  567.8 1.7 multiply_subtract_fusion.1
  569.5 138.9 %all-to-all-done.2 = bf16[64,10,2048]{2,1,0:T(8,128)(2,1)} async-done(((bf16[64,10,2048]{2,1,0:T(8,128)(2,1)}), bf16[64,10,2048]{2,1,0:T(8,128)(2,1)}, u32[]{:S(2)}, u32[]{:S(2)}) %all-to-all-start.2) | async-done | bytes 2621472 | tf_op jit(solution)/shard_map/all_to_all | solution.py:88
  708.4 2.9 convert_reduce_fusion
  711.3 0.1 reshape.51
  711.4 0.7 gather_fusion
  712.2 0.8 select_convert_fusion
  (2 shorter events, 0.0 us)
Async XLA Ops:
  7.2 2.4 copy-start
  12.4 64.7 %copy-start.3 = (f32[64]{0:T(128)S(1)}, f32[64]{0:T(128)}, u32[]{:S(2)}) copy-start(f32[64]{0:T(128)} %param.9) | copy-start | bytes 772
  12.4 203.2 %all-to-all-start.1 = ((bf16[64,10,2048]{2,1,0:T(8,128)(2,1)}), bf16[64,10,2048]{2,1,0:T(8,128)(2,1)}, u32[]{:S(2)}, u32[]{:S(2)}) async-start(bf16[64,10,2048]{2,1,0:T(8,128)(2,1)} %bitcast.17), calls=%async_computation.2 | async-start | bytes 8388608 | tf_op jit(solution)/shard_map/all_to_all | solution.py:78
  31.9 45.2 %reduce-scatter.4.cloned.1.call-start = ((), (), s32[]{:S(2)}) async-start(), calls=%async_computation.6 | async-start | bytes 2359296 | tf_op jit(solution)/shard_map/reduce_scatter | solution.py:44
  218.2 12.1 %copy-start.1 = (f32[256,320]{0,1:T(8,128)S(1)}, f32[256,320]{0,1:T(8,128)}, u32[]{:S(2)}) copy-start(f32[256,320]{0,1:T(8,128)} %param.10) | copy-start | bytes 983044
  218.2 195.7 %all-to-all-start = ((bf16[64,10,2048]{2,1,0:T(8,128)(2,1)}), bf16[64,10,2048]{2,1,0:T(8,128)(2,1)}, u32[]{:S(2)}, u32[]{:S(2)}) async-start(bf16[64,10,2048]{2,1,0:T(8,128)(2,1)} %bitcast.16), calls=%async_computation.1 | async-start | bytes 8388608 | tf_op jit(solution)/shard_map/all_to_all | solution.py:79
  230.2 37.6 %all-gather.5.cloned.1.call-start = ((), (), s32[]{:S(2)}) async-start(), calls=%async_computation.8 | async-start | bytes 1474560 | tf_op jit(solution)/shard_map/all_gather | solution.py:73
  231.0 229.5 %reduce-scatter.8.cloned.1.call-start = ((), (), s32[]{:S(2)}) async-start(), calls=%async_computation.10 | async-start | bytes 1474560 | tf_op jit(solution)/shard_map/reduce_scatter | solution.py:109
  419.4 41.1 %copy-start.2 = (f32[256,320]{0,1:T(8,128)S(1)}, f32[256,320]{0,1:T(8,128)}, u32[]{:S(2)}) copy-start(f32[256,320]{0,1:T(8,128)} %param.11) | copy-start | bytes 983044
  423.8 72.3 %all-gather.3.cloned.1.call-start = ((), (), s32[]{:S(2)}) async-start(), calls=%async_computation.7 | async-start | bytes 1474560 | tf_op jit(solution)/shard_map/all_gather | solution.py:74
  496.2 4.8 copy-start.4
  500.2 0.8 copy-start.5
  509.4 199.0 %all-to-all-start.2 = ((bf16[64,10,2048]{2,1,0:T(8,128)(2,1)}), bf16[64,10,2048]{2,1,0:T(8,128)(2,1)}, u32[]{:S(2)}, u32[]{:S(2)}) async-start(bf16[64,10,2048]{2,1,0:T(8,128)(2,1)} %reshape.50), calls=%async_computation.3 | async-start | bytes 8388608 | tf_op jit(solution)/shard_map/all_to_all | solution.py:88
  524.9 42.9 %reduce-scatter.6.cloned.1.call-start = ((), (), s32[]{:S(2)}) async-start(), calls=%async_computation.9 | async-start | bytes 1474560 | tf_op jit(solution)/shard_map/reduce_scatter | solution.py:102
Sparse Core Ops, SparseCore 0:
  35.6 41.5 reduce-scatter.3
  233.8 34.0 all-gather.4
  424.0 36.4 reduce-scatter.7
  463.0 33.1 all-gather.2
  528.3 39.4 reduce-scatter.5
where the time goes:
time: 726 us; the launch traced here: 720 us
  waiting for transfers between devices  607 us (84%)
  starting transfers between devices  47.2 us (7%)
  local copies, waits for them, and re-layouts  21.8 us (3%)
  matrix products  19.6 us (3%)
  between operations  13.9 us (2%)
  other arithmetic  10.2 us (1%)
    all_to_all x1, waiting for transfers between devices, shards(): lax.all_to_all(fan_out(gated), 'expert', split_axis=0, concat_axis=0, til...  143 us
    all_to_all x1, waiting for transfers between devices, shards(): lax.all_to_all(partial_x.reshape(n_expert, capacity, width), 'expert', sp...  139 us
    all_to_all x1, waiting for transfers between devices, shards(): lax.all_to_all(fan_out(tokens), 'expert', split_axis=0, concat_axis=0, ti...  137 us
    reduce_scatter x1, waiting for transfers between devices, summed_grads(): lax.psum_scatter(terms.astype(jnp.bfloat16), 'dp', scatter_dimension=0, t...  44.5 us
    reduce_scatter x1, waiting for transfers between devices, shards(): lax.psum_scatter((contract_rows(rows_part, pre_grad) * scale_in).astype(j...  39.6 us
    reduce_scatter x1, waiting for transfers between devices, shards(): lax.psum_scatter((contract_rows(rows_part, hidden) * scale_out).astype(jn...  36.6 us
    all_gather x1, waiting for transfers between devices, shards(): lax.all_gather(w_out.astype(jnp.bfloat16), 'dp', axis=0, tiled=True)  33.9 us
    all_gather x1, waiting for transfers between devices, shards(): lax.all_gather(w_in.astype(jnp.bfloat16), 'dp', axis=0, tiled=True)  32.7 us
  transfers between devices with their start and end apart: 8, of which 8 were waited for; matrix products, arithmetic and copies ran while one was open for 2% of the time, Pallas kernels for 0%

commit v1 on v0

v1 whole, which is shorter than its diff:
```python
import functools

import jax
import jax.numpy as jnp
from jax import lax
from jax.experimental import pallas as pl
from jax.experimental.pallas import tpu as pltpu
from jax.sharding import PartitionSpec as P

NX = 4
NY = 4
LINE = 4
BLOCKS = 4
CAP = 10
LANES = 128
MESH = pl.DeviceIdType.MESH

gelu_coef = 0.7978845608028654
cubic_coef = 0.044715
step_rate = 0.5
F32 = jnp.float32
BF16 = jnp.bfloat16


def add16(*terms):
    total = terms[0].astype(F32)
    for term in terms[1:]:
        total = total + term.astype(F32)
    return total.astype(BF16)


class Copies:
    def __init__(self, send_sems, recv_sems):
        self.send_sems = send_sems
        self.recv_sems = recv_sems
        self.count = 0
        self.started = []

    def start(self, src, dst, device):
        index = self.count
        self.count += 1
        copy = pltpu.make_async_remote_copy(
            src_ref=src,
            dst_ref=dst,
            send_sem=self.send_sems.at[index],
            recv_sem=self.recv_sems.at[index],
            device_id=device,
            device_id_type=MESH,
        )
        copy.start()
        self.started.append(copy)
        return copy

    def finish(self):
        for copy in self.started:
            copy.wait_send()


N_COPIES = 160


def kernel(
    dims,
    tok_ref, attn_ref, ids_ref, gate_ref, win_ref, wout_ref,
    tg_ref, nwin_ref, nwout_ref,
    pk_t, pk_g, x3, g3, x2, g2, perm, disp,
    wt, pre_slope, pg, hid, p2, p3,
    r1, m3, r3, r2, q3, rl, sb, slots,
    a_mate, a_sum, a_r1, a_m3, a_r3, a_r2,
    d_w, d_mate, d_sum, d_r1, d_m3, d_r3, d_r2,
    send_sems, recv_sems,
):
    width, hidden = dims
    scale_in = width ** (-0.5)
    scale_out = (hidden * NX * LINE) ** (-0.5)
    tiles = width // LANES
    expert = lax.axis_index("expert")
    dp = lax.axis_index("dp")
    z = expert // NX
    x = expert % NX
    block = z // LINE
    place = z % LINE
    y = dp // 2
    core = dp % 2
    rows_x = LINE * CAP
    rows_c = NX * rows_x

    right = (z * NX + (x + 1) % NX, dp)
    left = (z * NX + (x + NX - 1) % NX, dp)
    up = (expert, ((y + 1) % NY) * 2 + core)
    down = (expert, ((y + NY - 1) % NY) * 2 + core)
    mate = (expert, y * 2 + (1 - core))

    def line(r):
        return ((block * LINE + (place + r) % LINE) * NX + x, dp)

    def twin(j):
        return ((((block + j) % BLOCKS) * LINE + place) * NX + x, dp)

    barrier = pltpu.get_barrier_semaphore()
    partners = [right, left, up, down, mate]
    partners += [line(r) for r in range(1, LINE)] + [twin(j) for j in range(1, BLOCKS)]
    for device in partners:
        pl.semaphore_signal(barrier, inc=1, device_id=device, device_id_type=MESH)

    copies = Copies(send_sems, recv_sems)

    def at_row(c, xs, p):
        return c * rows_c + xs * rows_x + p * CAP

    row_i = lax.broadcasted_iota(jnp.int32, (256, 256), 0)
    col_i = lax.broadcasted_iota(jnp.int32, (256, 256), 1)
    perm[...] = jnp.where(col_i == (row_i % 16) * 16 + row_i // 16, 1.0, 0.0).astype(BF16)

    n_tok = tok_ref.shape[0]
    ids_row = ids_ref[...].astype(F32)
    eye_t = lax.broadcasted_iota(jnp.int32, (n_tok, n_tok), 0)
    eye_s = lax.broadcasted_iota(jnp.int32, (n_tok, n_tok), 1)
    spread_ids = jnp.broadcast_to(ids_row, (n_tok, n_tok))
    ids_col = jnp.sum(jnp.where(eye_t == eye_s, spread_ids, 0.0), axis=1, keepdims=True)
    earlier = jnp.where((ids_col == spread_ids) & (eye_t < eye_s), 1.0, 0.0)
    rank_row = jnp.sum(earlier, axis=0, keepdims=True)
    slot_row = jnp.where(rank_row < CAP, ids_row * CAP + rank_row, -1.0)
    n_slot = disp.shape[0]
    slot_i = lax.broadcasted_iota(jnp.int32, (n_slot, n_tok), 0).astype(F32)
    disp[...] = jnp.where(slot_i == jnp.broadcast_to(slot_row, (n_slot, n_tok)), 1.0, 0.0).astype(BF16)
    gate_col = jnp.sum(
        jnp.where(eye_t == eye_s, jnp.broadcast_to(gate_ref[...], (n_tok, n_tok)), 0.0),
        axis=1, keepdims=True,
    )

    def group_to_tiles(parts):
        return jnp.concatenate(parts, axis=0)

    def pack(rows, dst):
        packed = jnp.dot(disp[...], rows, preferred_element_type=F32).astype(BF16)
        for g in range(n_slot // 16):
            stacked = jnp.concatenate(
                [packed[g * 16:(g + 1) * 16, k * LANES:(k + 1) * LANES] for k in range(tiles)], axis=0
            )
            moved = jnp.dot(perm[...], stacked, preferred_element_type=F32).astype(BF16)
            dst[g * 16:(g + 1) * 16] = moved.reshape(16, tiles, LANES)

    def to_wide(src, dst, base, groups):
        def body(i, carry):
            first = base + i * 32
            pair = [src[pl.ds(first + h * 16, 16)].reshape(256, LANES) for h in range(2)]
            moved = jnp.dot(perm[...], jnp.concatenate(pair, axis=1), preferred_element_type=F32).astype(BF16)
            for h in range(2):
                at = pl.ds(pl.multiple_of(first + h * 16, 16), 16)
                for k in range(tiles):
                    dst[k // 2, at, (k % 2) * LANES:(k % 2 + 1) * LANES] = moved[
                        k * 16:(k + 1) * 16, h * LANES:(h + 1) * LANES
                    ]
            return carry

        lax.fori_loop(0, groups, body, 0)

    def to_narrow(src, dst, base, groups):
        def body(i, carry):
            pair = []
            for h in range(2):
                at = pl.ds(pl.multiple_of(i * 32 + h * 16, 16), 16)
                pair.append(jnp.concatenate(
                    [src[k // 2, at, (k % 2) * LANES:(k % 2 + 1) * LANES] for k in range(tiles)], axis=0
                ))
            moved = jnp.dot(perm[...], jnp.concatenate(pair, axis=1), preferred_element_type=F32).astype(BF16)
            for h in range(2):
                dst[pl.ds(base + i * 32 + h * 16, 16)] = moved[:, h * LANES:(h + 1) * LANES].reshape(16, tiles, LANES)
            return carry

        lax.fori_loop(0, groups, body, 0)

    pack(tok_ref[...], pk_t)
    own = at_row(block, x, place)
    x3[pl.ds(own, CAP)] = pk_t[pl.ds(block * CAP, CAP)]
    for half, source in ((0, win_ref), (1, wout_ref)):
        wt[dp, half * hidden:(half + 1) * hidden] = source[...].T.astype(BF16)
    slots[BLOCKS * CAP:] = jnp.zeros((slots.shape[0] - BLOCKS * CAP, tiles, LANES), BF16)

    pl.semaphore_wait(barrier, len(partners))

    def halves(count):
        return (pl.ds(0, count // 2), pl.ds(count // 2, count // 2))

    def pair_send(source, target):
        sent = {}
        for q in (2, 1, 3, 0):
            at = (y + q) % NY
            sent[q] = copies.start(source(at, 1 - core), target.at[at], mate)
        return sent

    def ring_begin(sent, source, mate_buf, sums, buf1, buf2, upper, lower):
        count = sums.shape[1]
        low, high = halves(count)
        started = {}
        for q in (2, 1, 3, 0):
            at = (y + q) % NY
            sent[q].wait_recv()
            sums[at] = add16(source(at, core)[...], mate_buf[at])
            if q == 2:
                started["u1"] = copies.start(sums.at[at, low], buf1.at[0], upper)
                started["d1"] = copies.start(sums.at[at, high], buf1.at[1], lower)
            elif q == 1:
                started["u2"] = copies.start(sums.at[at, high], buf2.at[0], upper)
            elif q == 3:
                started["d2"] = copies.start(sums.at[at, low], buf2.at[1], lower)
        return started

    def ring_middle(started, sums, buf1, mid, buf3, upper, lower):
        low, high = halves(sums.shape[1])
        started["u1"].wait_recv()
        mid[0] = add16(buf1[0], sums[(y + 1) % NY, low])
        started["u3"] = copies.start(mid.at[0], buf3.at[0], upper)
        started["d1"].wait_recv()
        mid[1] = add16(buf1[1], sums[(y + NY - 1) % NY, high])
        started["d3"] = copies.start(mid.at[1], buf3.at[1], lower)

    def ring_end(started, sums, buf2, buf3):
        low, high = halves(sums.shape[1])
        started["d2"].wait_recv()
        started["u3"].wait_recv()
        first = sums[y, low].astype(F32) + buf2[1].astype(F32) + buf3[0].astype(F32)
        started["u2"].wait_recv()
        started["d3"].wait_recv()
        second = sums[y, high].astype(F32) + buf2[0].astype(F32) + buf3[1].astype(F32)
        return first, second

    def attn_block(at, parity):
        return attn_ref.at[at, parity]

    def z_begin(packed, rows):
        spread = {0: [], }
        for r in range(1, LINE):
            spread[0].append(copies.start(packed.at[pl.ds(block * CAP, CAP)], rows.at[pl.ds(own, CAP)], line(r)))
        far = {}
        for j in (1, 3, 2):
            to = (block + j) % BLOCKS
            far[j] = copies.start(packed.at[pl.ds(to * CAP, CAP)], rows.at[pl.ds(own, CAP)], twin(j))
        return spread, far

    def chunk(j):
        return (block + BLOCKS - j) % BLOCKS

    def z_relay(state, rows, j):
        spread, far = state
        far[j].wait_recv()
        at = pl.ds(at_row(chunk(j), x, place), CAP)
        spread[j] = [copies.start(rows.at[at], rows.at[at], line(r)) for r in range(1, LINE)]

    def x_begin(state, rows, j):
        for copy in state[0][j]:
            copy.wait_recv()
        at = pl.ds(at_row(chunk(j), x, 0), rows_x)
        return [copies.start(rows.at[at], rows.at[at], device) for device in (right, left)]

    def x_forward(sent, rows, j):
        half = rows_x // 2
        sent[0].wait_recv()
        at = pl.ds(at_row(chunk(j), (x + NX - 1) % NX, 0), half)
        to_right = copies.start(rows.at[at], rows.at[at], right)
        sent[1].wait_recv()
        at = pl.ds(at_row(chunk(j), (x + 1) % NX, 0) + half, half)
        to_left = copies.start(rows.at[at], rows.at[at], left)
        return [to_right, to_left]

    def weights_begin():
        at = wt.at[dp]
        return [copies.start(at, at, device) for device in (up, down, mate)]

    def weights_middle(sent):
        low, high = halves(2 * hidden)
        below = ((y + NY - 1) % NY) * 2 + core
        above = ((y + 1) % NY) * 2 + core
        sent[0].wait_recv()
        to_up = copies.start(wt.at[below, low], wt.at[below, low], up)
        to_mate = [copies.start(wt.at[below], wt.at[below], mate)]
        sent[1].wait_recv()
        to_down = copies.start(wt.at[above, high], wt.at[above, high], down)
        to_mate.append(copies.start(wt.at[above], wt.at[above], mate))
        return [to_up, to_down], to_mate

    def weights_end(ends, to_mate):
        low, high = halves(2 * hidden)
        far = ((y + 2) % NY) * 2 + core
        for copy, part in zip(ends, (low, high)):
            copy.wait_recv()
            to_mate.append(copies.start(wt.at[far, part], wt.at[far, part], mate))

    def wide_dot(wide, rows, first):
        total = None
        for k in range(width // 256):
            term = lax.dot_general(
                wide[k, rows], wt[k, first:first + hidden],
                (((1,), (1,)), ((), ())), preferred_element_type=F32,
            )
            total = term if total is None else total + term
        return total

    def forward_chunk(j):
        base = chunk(j) * rows_c
        to_wide(x3, x2, base, rows_c // 32)
        rows = pl.ds(pl.multiple_of(base, 32), rows_c)
        pre = wide_dot(x2, rows, 0) * scale_in
        square = pre * pre
        tangent = jnp.tanh(gelu_coef * (pre + cubic_coef * square * pre))
        hid[rows] = (0.5 * pre * (1.0 + tangent)).astype(BF16)
        pre_slope[rows] = 0.5 * (1.0 + tangent) + 0.5 * pre * (1.0 - tangent * tangent) * gelu_coef * (
            1.0 + 3.0 * cubic_coef * square
        )

    def backward_chunk(j):
        base = chunk(j) * rows_c
        to_wide(g3, g2, base, rows_c // 32)
        rows = pl.ds(pl.multiple_of(base, 32), rows_c)
        grad = (wide_dot(g2, rows, hidden) * scale_out * pre_slope[rows]).astype(BF16)
        pg[rows] = grad
        for k in range(width // 256):
            p2[k] = (jnp.dot(grad, wt[k, 0:hidden], preferred_element_type=F32) * scale_in).astype(BF16)
        to_narrow(p2, p3, base, rows_c // 32)

    half = rows_x // 2

    def p_rows(j, xs, second, count):
        return pl.ds(at_row(chunk(j), xs % NX, 0) + second * half, count)

    def back_begin(j):
        out = {}
        out["r1"] = copies.start(p3.at[p_rows(j, x + 2, 0, half)], r1.at[j, 0], right)
        out["l1"] = copies.start(p3.at[p_rows(j, x + 2, 1, half)], r1.at[j, 1], left)
        out["r2"] = copies.start(p3.at[p_rows(j, x + 1, 1, half)], r2.at[j, 0], right)
        out["l2"] = copies.start(p3.at[p_rows(j, x + NX - 1, 0, half)], r2.at[j, 1], left)
        return out

    def back_middle(out, j):
        out["r1"].wait_recv()
        m3[j, 0] = add16(r1[j, 0], p3[p_rows(j, x + 1, 0, half)])
        out["r3"] = copies.start(m3.at[j, 0], r3.at[j, 0], right)
        out["l1"].wait_recv()
        m3[j, 1] = add16(r1[j, 1], p3[p_rows(j, x + NX - 1, 1, half)])
        out["l3"] = copies.start(m3.at[j, 1], r3.at[j, 1], left)

    def back_line(out, j):
        out["l2"].wait_recv()
        out["r3"].wait_recv()
        q3[j, 0:half] = add16(p3[p_rows(j, x, 0, half)], r3[j, 0], r2[j, 1])
        out["r2"].wait_recv()
        out["l3"].wait_recv()
        q3[j, half:rows_x] = add16(p3[p_rows(j, x, 1, half)], r2[j, 0], r3[j, 1])
        out["z"] = []
        for r in range(1, LINE):
            at = ((place + r) % LINE) * CAP
            out["z"].append(copies.start(q3.at[j, pl.ds(at, CAP)], rl.at[j, r - 1], line(r)))

    def back_far(out, j):
        for copy in out["z"]:
            copy.wait_recv()
        total = add16(q3[j, pl.ds(place * CAP, CAP)], rl[j, 0], rl[j, 1], rl[j, 2])
        at = pl.ds(block * CAP, CAP)
        if j == 0:
            slots[at] = total
        else:
            sb[j - 1] = total
            out["far"] = copies.start(sb.at[j - 1], slots.at[at], twin(BLOCKS - j))

    order = (0, 1, 3, 2)
    attn_sent = pair_send(attn_block, a_mate)
    t_state = z_begin(pk_t, x3)
    attn_ring = ring_begin(attn_sent, attn_block, a_mate, a_sum, a_r1, a_r2, up, down)
    w_first = weights_begin()
    t_x, t_f, g_x, g_f = {}, {}, {}, {}
    t_x[0] = x_begin(t_state, x3, 0)
    z_relay(t_state, x3, 1)
    ring_middle(attn_ring, a_sum, a_r1, a_m3, a_r3, up, down)
    z_relay(t_state, x3, 3)
    t_f[0] = x_forward(t_x[0], x3, 0)
    t_x[1] = x_begin(t_state, x3, 1)
    first, second = ring_end(attn_ring, a_sum, a_r2, a_r3)
    summed = jnp.concatenate([first, second], axis=0)
    pack((gate_col * summed).astype(BF16), pk_g)
    g3[pl.ds(own, CAP)] = pk_g[pl.ds(block * CAP, CAP)]
    g_state = z_begin(pk_g, g3)
    z_relay(t_state, x3, 2)
    t_x[3] = x_begin(t_state, x3, 3)
    t_f[1] = x_forward(t_x[1], x3, 1)
    w_ends, w_mate = weights_middle(w_first)
    t_x[2] = x_begin(t_state, x3, 2)
    t_f[3] = x_forward(t_x[3], x3, 3)
    g_x[0] = x_begin(g_state, g3, 0)
    z_relay(g_state, g3, 1)
    t_f[2] = x_forward(t_x[2], x3, 2)
    weights_end(w_ends, w_mate)
    z_relay(g_state, g3, 3)
    for copy in [w_first[2]] + w_mate:
        copy.wait_recv()
    g_x[1] = x_begin(g_state, g3, 1)
    z_relay(g_state, g3, 2)

    def arrive(copies_in):
        for copy in copies_in:
            copy.wait_recv()

    arrive(t_f[0])
    forward_chunk(0)
    g_f[0] = x_forward(g_x[0], g3, 0)
    g_x[3] = x_begin(g_state, g3, 3)
    arrive(t_f[1])
    forward_chunk(1)
    g_f[1] = x_forward(g_x[1], g3, 1)
    g_x[2] = x_begin(g_state, g3, 2)
    arrive(t_f[3])
    forward_chunk(3)
    g_f[3] = x_forward(g_x[3], g3, 3)
    arrive(t_f[2])
    forward_chunk(2)
    g_f[2] = x_forward(g_x[2], g3, 2)

    back = {}
    previous = None
    for j in order:
        arrive(g_f[j])
        backward_chunk(j)
        back[j] = back_begin(j)
        if previous is not None:
            back_middle(back[previous], previous)
        previous = j
    back_line(back[0], 0)
    back_middle(back[2], 2)
    back_line(back[1], 1)
    back_far(back[0], 0)

    grad_t = pg[...].T
    hid_t = hid[...].T

    def weight_grads(parity):
        def body(i, carry):
            k = i * 2 + parity
            d_w[i, parity, 0:hidden] = (
                jnp.dot(grad_t, x2[k], preferred_element_type=F32) * scale_in
            ).astype(BF16)
            d_w[i, parity, hidden:2 * hidden] = (
                jnp.dot(hid_t, g2[k], preferred_element_type=F32) * scale_out
            ).astype(BF16)
            return carry

        lax.fori_loop(0, NY, body, 0)

    def grad_block(at, parity):
        return d_w.at[at, parity]

    weight_grads(1 - core)
    d_sent = pair_send(grad_block, d_mate)
    back_line(back[3], 3)
    back_far(back[1], 1)
    weight_grads(core)
    d_ring = ring_begin(d_sent, grad_block, d_mate, d_sum, d_r1, d_r2, up, down)
    back_line(back[2], 2)
    back_far(back[3], 3)
    ring_middle(d_ring, d_sum, d_r1, d_m3, d_r3, up, down)
    back_far(back[2], 2)
    grad_in, grad_out = ring_end(d_ring, d_sum, d_r2, d_r3)
    nwin_ref[...] = win_ref[...] - step_rate * grad_in.T
    nwout_ref[...] = wout_ref[...] - step_rate * grad_out.T
    for j in (1, 3, 2):
        back[j]["far"].wait_recv()
    wide = []
    for g in range(n_slot // 16):
        moved = jnp.dot(
            perm[...], slots[g * 16:(g + 1) * 16].reshape(256, LANES), preferred_element_type=F32
        ).astype(BF16)
        wide.append(jnp.concatenate([moved[k * 16:(k + 1) * 16] for k in range(tiles)], axis=1))
    slots_wide = jnp.concatenate(wide, axis=0)
    tg_ref[...] = lax.dot_general(
        disp[...], slots_wide, (((0,), (0,)), ((), ())), preferred_element_type=F32
    ).astype(BF16)
    copies.finish()


def shards(tokens, attn_partials, expert_ids, gate, w_in, w_out):
    n_tok, width = tokens.shape
    hidden = w_in.shape[1]
    tiles = width // LANES
    rows = NX * LINE * BLOCKS * CAP
    rows_x = LINE * CAP
    half = rows_x // 2
    slot_rows = 48
    vmem = pl.BlockSpec(memory_space=pltpu.VMEM)

    def rows16(*lead):
        return pltpu.VMEM(lead + (tiles, LANES), BF16)

    def wide(*lead):
        return pltpu.VMEM(lead + (256,), BF16)

    parts = width // 256
    scratch = [
        rows16(slot_rows), rows16(slot_rows), rows16(rows), rows16(rows),
        wide(parts, rows), wide(parts, rows),
        pltpu.VMEM((256, 256), BF16), pltpu.VMEM((slot_rows, n_tok), BF16),
        wide(parts, 2 * hidden),
        pltpu.VMEM((rows, hidden), F32), pltpu.VMEM((rows, hidden), BF16), pltpu.VMEM((rows, hidden), BF16),
        wide(parts, rows // BLOCKS), rows16(rows),
        rows16(BLOCKS, 2, half), rows16(BLOCKS, 2, half), rows16(BLOCKS, 2, half), rows16(BLOCKS, 2, half),
        rows16(BLOCKS, rows_x), rows16(BLOCKS, LINE - 1, CAP), rows16(BLOCKS - 1, CAP), rows16(slot_rows),
        pltpu.VMEM((NY, n_tok, width), BF16), pltpu.VMEM((NY, n_tok, width), BF16),
    ]
    scratch += [pltpu.VMEM((2, n_tok // 2, width), BF16)] * 4
    scratch += [wide(NY, 2, 2 * hidden), wide(NY, 2 * hidden), wide(NY, 2 * hidden)]
    scratch += [wide(2, hidden)] * 4
    scratch += [pltpu.SemaphoreType.DMA((N_COPIES,)), pltpu.SemaphoreType.DMA((N_COPIES,))]
    return pl.pallas_call(
        functools.partial(kernel, (width, hidden)),
        out_shape=(
            jax.ShapeDtypeStruct((n_tok, width), BF16),
            jax.ShapeDtypeStruct(w_in.shape, F32),
            jax.ShapeDtypeStruct(w_out.shape, F32),
        ),
        in_specs=[vmem] * 6,
        out_specs=(vmem, vmem, vmem),
        scratch_shapes=scratch,
        compiler_params=pltpu.CompilerParams(
            collective_id=0, has_side_effects=True, vmem_limit_bytes=60 * 1024 * 1024
        ),
    )(
        tokens,
        attn_partials.reshape(NY, 2, n_tok, width),
        expert_ids.reshape(1, n_tok),
        gate.reshape(1, n_tok),
        w_in,
        w_out,
    )


def solution(mesh):
    in_specs = (
        P(("expert", "dp"), None),
        P("dp", "expert", None),
        P(("expert", "dp")),
        P(("expert", "dp")),
        P("dp", "expert"),
        P("dp", "expert"),
    )
    out_specs = (P(("expert", "dp"), None), P("dp", "expert"), P("dp", "expert"))
    return jax.shard_map(shards, mesh=mesh, in_specs=in_specs, out_specs=out_specs, check_vma=False)
```

time: 726 us -> 138 us (0.19)
  the two profiles are of different devices: /device:TPU:1 before, /device:TPU:2 now
where the time goes in v1:
time: 138 us
  Pallas kernels  128 us (93%)
  local copies, waits for them, and re-layouts  9.17 us (7%)
    pallas_call x1, Pallas kernels, shards(): pl.pallas_call(functools.partial(kernel, (width, hidden)), out_shape=(jax...  128 us
    unnamed x3, local copies, waits for them, and re-layouts  5.43 us
    pallas_call x2, local copies, waits for them, and re-layouts, shards(): pl.pallas_call(functools.partial(kernel, (width, hidden)), out_shape=(jax...  3.74 us

profile of v1, /device:TPU:2, one launch (start us, length us, event | category | flops | bytes accessed | tf_op | source)
XLA Modules:
  0.0 138.0 jit_solution(3404827949401479101)
XLA Ops:
  0.6 1.9 %copy.9.win_ref = f32[256,320]{1,0:T(8,128)} copy(f32[256,320]{0,1:T(8,128)} %param.10) | data formatting | bytes 655360 | tf_op args[4]
  2.5 1.9 %copy.10.wout_ref = f32[256,320]{1,0:T(8,128)} copy(f32[256,320]{0,1:T(8,128)} %param.11) | data formatting | bytes 655360 | tf_op args[5]
  4.4 128.2 %shard_map.85 = (bf16[64,2048]{1,0:T(8,128)(2,1)}, f32[256,320]{1,0:T(8,128)}, f32[256,320]{1,0:T(8,128)}) custom-call(bf16[64,2048]{1,0:T(8,128)(2,1)} %tok_ref.1, bf16[4,2,64,2048]{3,2,1,0:T(8,128)(2,1)} %bitcast.3, s32[1,64]{1,0:T(1,128)} %bitcast.4, f32[1,64]{1,0:T(1,128)} %bitcast.5, f32[256,320]{1,0:T(8,128)} %copy.9.win_ref, f32[256,320]{1,0:T(8,128)} %copy.10.wout_ref), custom_call_target="tpu_custom_call" | custom-call | tf_op jit(solution)/shard_map/pallas_call | solution.py:511
  132.6 1.9 %copy.11 = f32[256,320]{0,1:T(8,128)} copy(f32[256,320]{1,0:T(8,128)} %get-tuple-element.4) | data formatting | bytes 655360 | tf_op jit(solution)/shard_map/pallas_call | solution.py:511
  134.4 1.9 %copy.12 = f32[256,320]{0,1:T(8,128)} copy(f32[256,320]{1,0:T(8,128)} %get-tuple-element.5) | data formatting | bytes 655360 | tf_op jit(solution)/shard_map/pallas_call | solution.py:511
  136.3 1.7 %copy.14 = bf16[64,2048]{1,0:T(8,128)(2,1)} copy(bf16[64,2048]{1,0:T(8,128)(2,1)} %get-tuple-element.9) | data formatting | bytes 524288

commit v2 on v1

v2 whole, which is shorter than its diff:
```python
import functools

import jax
import jax.numpy as jnp
from jax import lax
from jax.experimental import pallas as pl
from jax.experimental.pallas import tpu as pltpu
from jax.sharding import PartitionSpec as P

NX = 4
NY = 4
LINE = 4
BLOCKS = 4
CAP = 10
LANES = 128
MESH = pl.DeviceIdType.MESH

gelu_coef = 0.7978845608028654
cubic_coef = 0.044715
step_rate = 0.5
F32 = jnp.float32
BF16 = jnp.bfloat16


def add16(*terms):
    total = terms[0].astype(F32)
    for term in terms[1:]:
        total = total + term.astype(F32)
    return total.astype(BF16)


class Copies:
    def __init__(self, send_sems, recv_sems):
        self.send_sems = send_sems
        self.recv_sems = recv_sems
        self.count = 0
        self.started = []

    def start(self, src, dst, device):
        index = self.count
        self.count += 1
        copy = pltpu.make_async_remote_copy(
            src_ref=src,
            dst_ref=dst,
            send_sem=self.send_sems.at[index],
            recv_sem=self.recv_sems.at[index],
            device_id=device,
            device_id_type=MESH,
        )
        copy.start()
        self.started.append(copy)
        return copy

    def finish(self):
        for copy in self.started:
            copy.wait_send()


N_COPIES = 192


def kernel(
    dims,
    tok_ref, attn_ref, ids_ref, gate_ref, win_ref, wout_ref,
    tg_ref, nwin_ref, nwout_ref,
    pk_t, pk_g, x3, g3, x2, g2, perm, disp,
    w_stage, w_in, w_out, pre_slope, pg, hid, p2, p3, p_mate,
    q3, rl, sb, slots,
    a_mate, a_sum, a_r1, a_m3, a_r3, a_r2,
    d_in, i_r1, i_m3, i_r3, i_r2, i_sum, is_r1, is_m3, is_r3, is_r2,
    d_out, o_r1, o_m3, o_r3, o_r2, o_sum, os_r1, os_m3, os_r3, os_r2,
    d_part, d_other,
    send_sems, recv_sems,
):
    width, hidden = dims
    scale_in = width ** (-0.5)
    scale_out = (hidden * NX * LINE) ** (-0.5)
    tiles = width // LANES
    share = hidden // 2
    units = NX * share
    depth = width // NY
    expert = lax.axis_index("expert")
    dp = lax.axis_index("dp")
    z = expert // NX
    x = expert % NX
    block = z // LINE
    place = z % LINE
    y = dp // 2
    core = dp % 2
    rows_b = LINE * CAP
    rows_d = BLOCKS * rows_b

    right = (z * NX + (x + 1) % NX, dp)
    left = (z * NX + (x + NX - 1) % NX, dp)
    up = (expert, ((y + 1) % NY) * 2 + core)
    down = (expert, ((y + NY - 1) % NY) * 2 + core)
    mate = (expert, y * 2 + (1 - core))

    def line(r):
        return ((block * LINE + (place + r) % LINE) * NX + x, dp)

    def twin(j):
        return ((((block + j) % BLOCKS) * LINE + place) * NX + x, dp)

    barrier = pltpu.get_barrier_semaphore()
    partners = [right, left, up, down, mate]
    partners += [line(r) for r in range(1, LINE)] + [twin(j) for j in range(1, BLOCKS)]
    for device in partners:
        pl.semaphore_signal(barrier, inc=1, device_id=device, device_id_type=MESH)

    copies = Copies(send_sems, recv_sems)

    def arrive(*waiting):
        for copy in waiting:
            copy.wait_recv()

    row_i = lax.broadcasted_iota(jnp.int32, (256, 256), 0)
    col_i = lax.broadcasted_iota(jnp.int32, (256, 256), 1)
    perm[...] = jnp.where(col_i == (row_i % 16) * 16 + row_i // 16, 1.0, 0.0).astype(BF16)

    n_tok = tok_ref.shape[0]
    ids_row = ids_ref[...].astype(F32)
    eye_t = lax.broadcasted_iota(jnp.int32, (n_tok, n_tok), 0)
    eye_s = lax.broadcasted_iota(jnp.int32, (n_tok, n_tok), 1)
    spread_ids = jnp.broadcast_to(ids_row, (n_tok, n_tok))
    ids_col = jnp.sum(jnp.where(eye_t == eye_s, spread_ids, 0.0), axis=1, keepdims=True)
    earlier = jnp.where((ids_col == spread_ids) & (eye_t < eye_s), 1.0, 0.0)
    rank_row = jnp.sum(earlier, axis=0, keepdims=True)
    slot_row = jnp.where(rank_row < CAP, ids_row * CAP + rank_row, -1.0)
    n_slot = disp.shape[0]
    slot_i = lax.broadcasted_iota(jnp.int32, (n_slot, n_tok), 0).astype(F32)
    disp[...] = jnp.where(slot_i == jnp.broadcast_to(slot_row, (n_slot, n_tok)), 1.0, 0.0).astype(BF16)
    gate_col = jnp.sum(
        jnp.where(eye_t == eye_s, jnp.broadcast_to(gate_ref[...], (n_tok, n_tok)), 0.0),
        axis=1, keepdims=True,
    )

    def pack(rows, dst):
        packed = jnp.dot(disp[...], rows, preferred_element_type=F32).astype(BF16)
        for g in range(n_slot // 16):
            stacked = jnp.concatenate(
                [packed[g * 16:(g + 1) * 16, k * LANES:(k + 1) * LANES] for k in range(tiles)], axis=0
            )
            moved = jnp.dot(perm[...], stacked, preferred_element_type=F32).astype(BF16)
            dst[g * 16:(g + 1) * 16] = moved.reshape(16, tiles, LANES)

    per = depth // LANES

    def to_wide(src, dst, half):
        def body(i, carry):
            pair = [src[half, pl.ds(i * 32 + h * 16, 16)].reshape(256, LANES) for h in range(2)]
            moved = jnp.dot(perm[...], jnp.concatenate(pair, axis=1), preferred_element_type=F32).astype(BF16)
            for h in range(2):
                at = pl.ds(pl.multiple_of(half * rows_d + i * 32 + h * 16, 16), 16)
                for k in range(tiles):
                    dst[k // per, at, (k % per) * LANES:(k % per + 1) * LANES] = moved[
                        k * 16:(k + 1) * 16, h * LANES:(h + 1) * LANES
                    ]
            return carry

        lax.fori_loop(0, rows_d // 32, body, 0)

    def to_narrow(src, dst, half):
        def body(i, carry):
            pair = []
            for h in range(2):
                at = pl.ds(pl.multiple_of(i * 32 + h * 16, 16), 16)
                pair.append(jnp.concatenate(
                    [src[k // per, at, (k % per) * LANES:(k % per + 1) * LANES] for k in range(tiles)], axis=0
                ))
            moved = jnp.dot(perm[...], jnp.concatenate(pair, axis=1), preferred_element_type=F32).astype(BF16)
            for h in range(2):
                dst[half, pl.ds(i * 32 + h * 16, 16)] = moved[:, h * LANES:(h + 1) * LANES].reshape(16, tiles, LANES)
            return carry

        lax.fori_loop(0, rows_d // 32, body, 0)

    pack(tok_ref[...], pk_t)

    def row_at(c, p):
        return c * rows_b + p * CAP

    own = row_at(block, place)
    x3[core, pl.ds(own, CAP)] = pk_t[pl.ds(block * CAP, CAP)]
    mine = pl.ds(pl.multiple_of(core * share, share), share)
    other = pl.ds(pl.multiple_of((1 - core) * share, share), share)
    lanes_mine = pl.ds(pl.multiple_of(core * (depth // 2), depth // 2), depth // 2)
    lanes_other = pl.ds(pl.multiple_of((1 - core) * (depth // 2), depth // 2), depth // 2)
    w_in[y, x, :, lanes_mine] = win_ref[mine].astype(BF16)
    w_out[x, y, :, lanes_mine] = wout_ref[mine].astype(BF16)
    w_stage[0] = win_ref[other].astype(BF16)
    w_stage[1] = wout_ref[other].astype(BF16)
    slots[BLOCKS * CAP:] = jnp.zeros((slots.shape[0] - BLOCKS * CAP, tiles, LANES), BF16)

    pl.semaphore_wait(barrier, len(partners))

    def halves(count):
        return pl.ds(0, count // 2), pl.ds(count // 2, count // 2)

    X_RING = (x, right, left)
    Y_RING = (y, up, down)

    def gather_first(blk, ring):
        pos, upper, lower = ring
        return [copies.start(blk(pos), blk(pos), device) for device in (upper, lower)]

    def gather_next(sent, blk, ring):
        pos, upper, lower = ring
        low, high = halves(share)
        below, above = (pos + 3) % 4, (pos + 1) % 4
        sent[0].wait_recv()
        to_up = copies.start(blk(below).at[low], blk(below).at[low], upper)
        sent[1].wait_recv()
        to_down = copies.start(blk(above).at[high], blk(above).at[high], lower)
        return [to_up, to_down]

    def scatter_first(blk, count, buf1, buf2, ring):
        pos, upper, lower = ring
        low, high = halves(count)
        far, above, below = (pos + 2) % 4, (pos + 1) % 4, (pos + 3) % 4
        return {
            "u1": copies.start(blk(far).at[low], buf1.at[0], upper),
            "d1": copies.start(blk(far).at[high], buf1.at[1], lower),
            "u2": copies.start(blk(above).at[high], buf2.at[0], upper),
            "d2": copies.start(blk(below).at[low], buf2.at[1], lower),
        }

    def scatter_middle(sent, blk, count, buf1, mid, buf3, ring):
        pos, upper, lower = ring
        low, high = halves(count)
        sent["u1"].wait_recv()
        mid[0] = add16(buf1[0], blk((pos + 1) % 4).at[low][...])
        sent["u3"] = copies.start(mid.at[0], buf3.at[0], upper)
        sent["d1"].wait_recv()
        mid[1] = add16(buf1[1], blk((pos + 3) % 4).at[high][...])
        sent["d3"] = copies.start(mid.at[1], buf3.at[1], lower)

    def scatter_end(sent, blk, count, buf2, buf3, ring):
        low, high = halves(count)
        pos = ring[0]
        arrive(sent["d2"], sent["u3"])
        first = blk(pos).at[low][...].astype(F32) + buf2[1].astype(F32) + buf3[0].astype(F32)
        arrive(sent["u2"], sent["d3"])
        second = blk(pos).at[high][...].astype(F32) + buf2[0].astype(F32) + buf3[1].astype(F32)
        return first, second

    def attn_begin(sent):
        low, high = halves(n_tok)
        out = {}
        for q in (2, 1, 3, 0):
            at = (y + q) % NY
            sent[q].wait_recv()
            a_sum[at] = add16(attn_ref[at, core], a_mate[at])
            if q == 2:
                out["u1"] = copies.start(a_sum.at[at, low], a_r1.at[0], up)
                out["d1"] = copies.start(a_sum.at[at, high], a_r1.at[1], down)
            elif q == 1:
                out["u2"] = copies.start(a_sum.at[at, high], a_r2.at[0], up)
            elif q == 3:
                out["d2"] = copies.start(a_sum.at[at, low], a_r2.at[1], down)
        return out

    def z_begin(packed, rows):
        at = pl.ds(block * CAP, CAP)
        spread = {0: [copies.start(packed.at[at], rows.at[core, pl.ds(own, CAP)], line(r)) for r in range(1, LINE)]}
        far = {}
        for j in (1, 3, 2):
            to = (block + j) % BLOCKS
            far[j] = copies.start(packed.at[pl.ds(to * CAP, CAP)], rows.at[core, pl.ds(own, CAP)], twin(j))
        return spread, far

    def chunk(j):
        return (block + BLOCKS - j) % BLOCKS

    def z_relay(state, rows, j):
        spread, far = state
        far[j].wait_recv()
        at = pl.ds(row_at(chunk(j), place), CAP)
        spread[j] = [copies.start(rows.at[core, at], rows.at[core, at], line(r)) for r in range(1, LINE)]

    def z_share(state, rows, j):
        arrive(*state[0][j])
        at = pl.ds(row_at(chunk(j), 0), rows_b)
        return copies.start(rows.at[core, at], rows.at[core, at], mate)

    def back_share(j):
        at = pl.ds(row_at(chunk(j), 0), rows_b)
        return {"m": copies.start(p3.at[1 - core, at], p_mate.at[at], mate)}

    def back_line(out, j):
        at = pl.ds(row_at(chunk(j), 0), rows_b)
        out["m"].wait_recv()
        q3[j] = add16(p3[core, at], p_mate[at])
        out["z"] = []
        for r in range(1, LINE):
            to = ((place + r) % LINE) * CAP
            out["z"].append(copies.start(q3.at[j, pl.ds(to, CAP)], rl.at[j, r - 1], line(r)))

    def back_far(out, j):
        arrive(*out["z"])
        total = add16(q3[j, pl.ds(place * CAP, CAP)], rl[j, 0], rl[j, 1], rl[j, 2])
        at = pl.ds(block * CAP, CAP)
        if j == 0:
            slots[at] = total
        else:
            sb[j - 1] = total
            out["far"] = copies.start(sb.at[j - 1], slots.at[at], twin(BLOCKS - j))

    def in_x(i):
        return w_in.at[y, i]

    def out_y(i):
        return w_out.at[x, i]

    def in_y(s):
        return lambda i: w_in.at[i, s]

    def out_x(s):
        return lambda i: w_out.at[i, s]

    w_pair = [
        copies.start(w_stage.at[0], w_in.at[y, x, :, lanes_mine], mate),
        copies.start(w_stage.at[1], w_out.at[x, y, :, lanes_mine], mate),
    ]
    attn_sent = {}
    for q in (2, 1, 3, 0):
        at = (y + q) % NY
        attn_sent[q] = copies.start(attn_ref.at[at, 1 - core], a_mate.at[at], mate)
    t_state = z_begin(pk_t, x3)
    arrive(w_pair[0])
    in_first = gather_first(in_x, X_RING)
    attn_ring = attn_begin(attn_sent)
    arrive(w_pair[1])
    out_first = gather_first(out_y, Y_RING)
    in_big, out_big = {}, {}
    in_big[0] = gather_first(in_y(x), Y_RING)
    out_big[0] = gather_first(out_x(y), X_RING)
    z_relay(t_state, x3, 1)
    in_next = gather_next(in_first, in_x, X_RING)
    for q in (1, 3):
        in_big[q] = gather_first(in_y((x + q) % NX), Y_RING)
    z_relay(t_state, x3, 3)
    a_low, a_high = halves(n_tok)
    scatter_middle(attn_ring, lambda i: a_sum.at[i], n_tok, a_r1, a_m3, a_r3, Y_RING)
    out_next = gather_next(out_first, out_y, Y_RING)
    for q in (1, 3):
        out_big[q] = gather_first(out_x((y + q) % NY), X_RING)
    z_relay(t_state, x3, 2)
    arrive(*in_next)
    in_big[2] = gather_first(in_y((x + 2) % NX), Y_RING)
    t_share = {0: z_share(t_state, x3, 0), 1: z_share(t_state, x3, 1)}
    first, second = scatter_end(attn_ring, lambda i: a_sum.at[i], n_tok, a_r2, a_r3, Y_RING)
    summed = jnp.concatenate([first, second], axis=0)
    pack((gate_col * summed).astype(BF16), pk_g)
    g3[core, pl.ds(own, CAP)] = pk_g[pl.ds(block * CAP, CAP)]
    g_state = z_begin(pk_g, g3)
    in_last, out_last = {}, {}
    in_last[0] = gather_next(in_big[0], in_y(x), Y_RING)
    arrive(*out_next)
    out_big[2] = gather_first(out_x((y + 2) % NY), X_RING)
    out_last[0] = gather_next(out_big[0], out_x(y), X_RING)
    t_share[3] = z_share(t_state, x3, 3)
    t_share[2] = z_share(t_state, x3, 2)
    for q in (1, 3):
        in_last[q] = gather_next(in_big[q], in_y((x + q) % NX), Y_RING)
        out_last[q] = gather_next(out_big[q], out_x((y + q) % NY), X_RING)
        z_relay(g_state, g3, q)
    in_last[2] = gather_next(in_big[2], in_y((x + 2) % NX), Y_RING)
    out_last[2] = gather_next(out_big[2], out_x((y + 2) % NY), X_RING)
    z_relay(g_state, g3, 2)
    g_share = {}
    g_share[0] = z_share(g_state, g3, 0)

    to_wide(x3, x2, core)
    arrive(*t_share.values())
    to_wide(x3, x2, 1 - core)
    for q in range(4):
        arrive(*in_last[q])
    pre = None
    for k in range(NY):
        term = lax.dot_general(
            x2[k], w_in[k].reshape(units, depth), (((1,), (1,)), ((), ())), preferred_element_type=F32
        )
        pre = term if pre is None else pre + term
    pre = pre * scale_in
    square = pre * pre
    tangent = jnp.tanh(gelu_coef * (pre + cubic_coef * square * pre))
    hid[...] = (0.5 * pre * (1.0 + tangent)).astype(BF16)
    pre_slope[...] = scale_out * (
        0.5 * (1.0 + tangent) + 0.5 * pre * (1.0 - tangent * tangent) * gelu_coef * (1.0 + 3.0 * cubic_coef * square)
    )
    for q in (1, 3, 2):
        g_share[q] = z_share(g_state, g3, q)
    hid_t = hid[...].T
    to_wide(g3, g2, core)
    arrive(*g_share.values())
    to_wide(g3, g2, 1 - core)

    for k in range(NY):
        grads = (jnp.dot(hid_t, g2[k], preferred_element_type=F32) * scale_out).astype(BF16)
        for i in range(NX):
            d_out[i, k] = grads[i * share:(i + 1) * share]
    out_ring = scatter_first(lambda i: d_out.at[i], NY, o_r1, o_r2, X_RING)

    for q in range(4):
        arrive(*out_last[q])
    total = None
    for k in range(NY):
        columns = jnp.concatenate([w_out[i, k] for i in range(NX)], axis=0)
        term = lax.dot_general(g2[k], columns, (((1,), (1,)), ((), ())), preferred_element_type=F32)
        total = term if total is None else total + term
    pg[...] = (total * pre_slope[...]).astype(BF16)

    back = {}
    order = (0, 1, 3, 2)
    for part in range(2):
        half = (1 - core) if part == 0 else core
        rows = pg[pl.ds(pl.multiple_of(half * rows_d, rows_d), rows_d)]
        for k in range(NY):
            p2[k] = (
                jnp.dot(rows, w_in[k].reshape(units, depth), preferred_element_type=F32) * scale_in
            ).astype(BF16)
        to_narrow(p2, p3, half)
        if part == 0:
            for j in order:
                back[j] = back_share(j)
    scatter_middle(out_ring, lambda i: d_out.at[i], NY, o_r1, o_m3, o_r3, X_RING)
    for j in order:
        back_line(back[j], j)
    pg_t = pg[...].T
    for k in range(NY):
        grads = (jnp.dot(pg_t, x2[k], preferred_element_type=F32) * scale_in).astype(BF16)
        d_in[k] = grads.reshape(NX, share, depth)
    in_ring = scatter_first(lambda i: d_in.at[i], NX, i_r1, i_r2, Y_RING)
    for j in order:
        back_far(back[j], j)
    scatter_middle(in_ring, lambda i: d_in.at[i], NX, i_r1, i_m3, i_r3, Y_RING)

    first, second = scatter_end(out_ring, lambda i: d_out.at[i], NY, o_r2, o_r3, X_RING)
    o_sum[0:2] = first.astype(BF16)
    o_sum[2:4] = second.astype(BF16)
    out_small = scatter_first(lambda i: o_sum.at[i], share, os_r1, os_r2, Y_RING)
    first, second = scatter_end(in_ring, lambda i: d_in.at[i], NX, i_r2, i_r3, Y_RING)
    i_sum[0:2] = first.astype(BF16)
    i_sum[2:4] = second.astype(BF16)
    in_small = scatter_first(lambda i: i_sum.at[i], share, is_r1, is_r2, X_RING)
    scatter_middle(out_small, lambda i: o_sum.at[i], share, os_r1, os_m3, os_r3, Y_RING)
    scatter_middle(in_small, lambda i: i_sum.at[i], share, is_r1, is_m3, is_r3, X_RING)
    pair = []
    for t, sent, sums, buf2, buf3, ring in (
        (1, out_small, o_sum, os_r2, os_r3, Y_RING), (0, in_small, i_sum, is_r2, is_r3, X_RING),
    ):
        low, high = halves(share)
        first, second = scatter_end(sent, lambda i: sums.at[i], share, buf2, buf3, ring)
        d_part[t, low] = first.astype(BF16)
        d_part[t, high] = second.astype(BF16)
        pair.append(copies.start(d_part.at[t, :, lanes_other], d_other.at[t], mate))

    arrive(back[1]["far"], back[3]["far"], back[2]["far"])
    wide = []
    for g in range(n_slot // 16):
        moved = jnp.dot(
            perm[...], slots[g * 16:(g + 1) * 16].reshape(256, LANES), preferred_element_type=F32
        ).astype(BF16)
        wide.append(jnp.concatenate([moved[k * 16:(k + 1) * 16] for k in range(tiles)], axis=1))
    slots_wide = jnp.concatenate(wide, axis=0)
    tg_ref[...] = lax.dot_general(
        disp[...], slots_wide, (((0,), (0,)), ((), ())), preferred_element_type=F32
    ).astype(BF16)

    for t, copy, old, new in ((1, pair[0], wout_ref, nwout_ref), (0, pair[1], win_ref, nwin_ref)):
        new[mine] = old[mine] - step_rate * d_part[t, :, lanes_mine].astype(F32)
        copy.wait_recv()
        new[other] = old[other] - step_rate * d_other[t].astype(F32)
    copies.finish()


def shards(tokens, attn_partials, expert_ids, gate, w_in, w_out):
    n_tok, width = tokens.shape
    w_in_t, w_out_t = w_in.T, w_out.T
    hidden = w_in_t.shape[0]
    tiles = width // LANES
    rows_b = LINE * CAP
    rows_d = BLOCKS * rows_b
    share = hidden // 2
    units = NX * share
    depth = width // NY
    slot_rows = 48
    vmem = pl.BlockSpec(memory_space=pltpu.VMEM)

    def bf16(*shape):
        return pltpu.VMEM(shape, BF16)

    def rows16(*lead):
        return bf16(*lead, tiles, LANES)

    scratch = [
        rows16(slot_rows), rows16(slot_rows), rows16(2, rows_d), rows16(2, rows_d),
        bf16(NY, 2 * rows_d, depth), bf16(NY, 2 * rows_d, depth),
        bf16(256, 256), bf16(slot_rows, n_tok),
        bf16(2, share, depth // 2), bf16(NY, NX, share, depth), bf16(NX, NY, share, depth),
        pltpu.VMEM((2 * rows_d, units), F32), bf16(2 * rows_d, units), bf16(2 * rows_d, units),
        bf16(NY, rows_d, depth), rows16(2, rows_d), rows16(rows_d),
        rows16(BLOCKS, rows_b), rows16(BLOCKS, LINE - 1, CAP), rows16(BLOCKS - 1, CAP), rows16(slot_rows),
        bf16(NY, n_tok, width), bf16(NY, n_tok, width),
    ]
    scratch += [bf16(2, n_tok // 2, width)] * 4
    for _ in range(2):
        scratch += [bf16(4, 4, share, depth)] + [bf16(2, 2, share, depth)] * 4
        scratch += [bf16(4, share, depth)] + [bf16(2, share // 2, depth)] * 4
    scratch += [bf16(2, share, depth), bf16(2, share, depth // 2)]
    scratch += [pltpu.SemaphoreType.DMA((N_COPIES,)), pltpu.SemaphoreType.DMA((N_COPIES,))]
    token_grad, new_in, new_out = pl.pallas_call(
        functools.partial(kernel, (width, hidden)),
        out_shape=(
            jax.ShapeDtypeStruct((n_tok, width), BF16),
            jax.ShapeDtypeStruct(w_in_t.shape, F32),
            jax.ShapeDtypeStruct(w_out_t.shape, F32),
        ),
        in_specs=[vmem] * 6,
        out_specs=(vmem, vmem, vmem),
        scratch_shapes=scratch,
        compiler_params=pltpu.CompilerParams(
            collective_id=0, has_side_effects=True, vmem_limit_bytes=60 * 1024 * 1024
        ),
    )(
        tokens,
        attn_partials.reshape(NY, 2, n_tok, width),
        expert_ids.reshape(1, n_tok),
        gate.reshape(1, n_tok),
        w_in_t,
        w_out_t,
    )
    return token_grad, new_in.T, new_out.T


def solution(mesh):
    in_specs = (
        P(("expert", "dp"), None),
        P("dp", "expert", None),
        P(("expert", "dp")),
        P(("expert", "dp")),
        P("dp", "expert"),
        P("dp", "expert"),
    )
    out_specs = (P(("expert", "dp"), None), P("dp", "expert"), P("dp", "expert"))
    return jax.shard_map(shards, mesh=mesh, in_specs=in_specs, out_specs=out_specs, check_vma=False)
```

time: 138 us -> 129 us (0.935)
  the two profiles are of different devices: /device:TPU:2 before, /device:TPU:1 now
where the time goes in v2:
time: 129 us
  Pallas kernels  123 us (95%)
  local copies, waits for them, and re-layouts  5.1 us (4%)
    pallas_call x1, Pallas kernels, shards(): pl.pallas_call(functools.partial(kernel, (width, hidden)), out_shape=(jax...  123 us
    unnamed x3, local copies, waits for them, and re-layouts  5.1 us

profile of v2, /device:TPU:1, one launch (start us, length us, event | category | flops | bytes accessed | tf_op | source)
XLA Modules:
  0.0 128.6 jit_solution(3325651056644416802)
XLA Ops:
  0.6 122.9 %shard_map.85 = (bf16[64,2048]{1,0:T(8,128)(2,1)}, f32[320,256]{1,0:T(8,128)}, f32[320,256]{1,0:T(8,128)}) custom-call(bf16[64,2048]{1,0:T(8,128)(2,1)} %tok_ref.1, bf16[4,2,64,2048]{3,2,1,0:T(8,128)(2,1)} %bitcast.7, s32[1,64]{1,0:T(1,128)} %bitcast.12, f32[1,64]{1,0:T(1,128)} %bitcast.13, f32[320,256]{1,0:T(8,128)} %bitcast.10, f32[320,256]{1,0:T(8,128)} %bitcast.11), custom_call_target="tpu_custom_call" | custom-call | tf_op jit(solution)/shard_map/pallas_call | solution.py:513
  123.5 1.7 %copy.12 = bf16[64,2048]{1,0:T(8,128)(2,1)} copy(bf16[64,2048]{1,0:T(8,128)(2,1)} %get-tuple-element.12) | data formatting | bytes 524288
  125.2 1.7 %copy.13 = f32[256,320]{0,1:T(8,128)} copy(f32[256,320]{0,1:T(8,128)} %bitcast.9) | data formatting | bytes 655360
  126.9 1.7 %copy.14 = f32[256,320]{0,1:T(8,128)} copy(f32[256,320]{0,1:T(8,128)} %bitcast.8) | data formatting | bytes 655360

commit v3 on v2

--- a/solution.py
+++ b/solution.py
@@ -29,34 +29,62 @@
     return total.astype(BF16)
 
 
+class Copy:
+    def __init__(self, copy, when):
+        self.copy = copy
+        self.when = when
+
+    def wait_recv(self, when=None):
+        guarded(when, self.copy.wait_recv)
+
+
+def guarded(when, action):
+    if when is None:
+        action()
+    else:
+        pl.when(when)(action)
+
+
 class Copies:
     def __init__(self, send_sems, recv_sems):
         self.send_sems = send_sems
         self.recv_sems = recv_sems
-        self.count = 0
+        self.sends = 0
+        self.recvs = 0
         self.started = []
 
-    def start(self, src, dst, device):
-        index = self.count
-        self.count += 1
-        copy = pltpu.make_async_remote_copy(
+    def slots(self, count):
+        first = self.recvs
+        self.recvs += count
+        return first
+
+    def make(self, src, dst, device, recv=None, send=None):
+        if recv is None:
+            recv = self.slots(1)
+        if send is None:
+            send = self.sends
+            self.sends += 1
+        return pltpu.make_async_remote_copy(
             src_ref=src,
             dst_ref=dst,
-            send_sem=self.send_sems.at[index],
-            recv_sem=self.recv_sems.at[index],
+            send_sem=self.send_sems.at[send],
+            recv_sem=self.recv_sems.at[recv],
             device_id=device,
             device_id_type=MESH,
         )
-        copy.start()
+
+    def start(self, src, dst, device, when=None, recv=None):
+        copy = Copy(self.make(src, dst, device, recv), when)
+        guarded(when, copy.copy.start)
         self.started.append(copy)
         return copy
 
     def finish(self):
         for copy in self.started:
-            copy.wait_send()
-
-
-N_COPIES = 192
+            guarded(copy.when, copy.copy.wait_send)
+
+
+N_COPIES = 384
 
 
 def kernel(
@@ -64,8 +92,8 @@
     tok_ref, attn_ref, ids_ref, gate_ref, win_ref, wout_ref,
     tg_ref, nwin_ref, nwout_ref,
     pk_t, pk_g, x3, g3, x2, g2, perm, disp,
-    w_stage, w_in, w_out, pre_slope, pg, hid, p2, p3, p_mate,
-    q3, rl, sb, slots,
+    w_stage, w_in, w_out, pre_slope, grad_sum, pg, pg_t, hid, p2, p3, p_mate,
+    q3, zr, zl, zs_r, zs_l, own_r, own_l, own_sr, own_sl, slots,
     a_mate, a_sum, a_r1, a_m3, a_r3, a_r2,
     d_in, i_r1, i_m3, i_r3, i_r2, i_sum, is_r1, is_m3, is_r3, is_r2,
     d_out, o_r1, o_m3, o_r3, o_r2, o_sum, os_r1, os_m3, os_r3, os_r2,
@@ -77,7 +105,6 @@
     scale_out = (hidden * NX * LINE) ** (-0.5)
     tiles = width // LANES
     share = hidden // 2
-    units = NX * share
     depth = width // NY
     expert = lax.axis_index("expert")
     dp = lax.axis_index("dp")
@@ -96,17 +123,32 @@
     down = (expert, ((y + NY - 1) % NY) * 2 + core)
     mate = (expert, y * 2 + (1 - core))
 
-    def line(r):
-        return ((block * LINE + (place + r) % LINE) * NX + x, dp)
-
-    def twin(j):
-        return ((((block + j) % BLOCKS) * LINE + place) * NX + x, dp)
+    last = LINE - 1
+    not_first, not_last = place > 0, place < last
+    at_first, at_last = place == 0, place == last
+    front = ((z + 1) % (BLOCKS * LINE) * NX + x, dp)
+    back_z = ((z + BLOCKS * LINE - 1) % (BLOCKS * LINE) * NX + x, dp)
+
+    def seat(step, at):
+        return ((((block + step + BLOCKS) % BLOCKS) * LINE + at) * NX + x, dp)
 
     barrier = pltpu.get_barrier_semaphore()
-    partners = [right, left, up, down, mate]
-    partners += [line(r) for r in range(1, LINE)] + [twin(j) for j in range(1, BLOCKS)]
-    for device in partners:
-        pl.semaphore_signal(barrier, inc=1, device_id=device, device_id_type=MESH)
+
+    def greet(device, when=None):
+        guarded(when, lambda: pl.semaphore_signal(barrier, inc=1, device_id=device, device_id_type=MESH))
+
+    for device in (right, left, up, down, mate):
+        greet(device)
+    greet(front, not_last)
+    greet(back_z, not_first)
+    for step in (1, 2):
+        greet(seat(step, 0))
+        greet(seat(-step, last))
+        for at in range(LINE):
+            greet(seat(step, at), at_last)
+            greet(seat(-step, at), at_first)
+    edge = jnp.where(at_first | at_last, 2 * LINE - 1, 0)
+    greetings = 5 + 2 + 4 + edge
 
     copies = Copies(send_sems, recv_sems)
 
@@ -180,8 +222,7 @@
     def row_at(c, p):
         return c * rows_b + p * CAP
 
-    own = row_at(block, place)
-    x3[core, pl.ds(own, CAP)] = pk_t[pl.ds(block * CAP, CAP)]
+    x3[core, pl.ds(row_at(block, place), CAP)] = pk_t[pl.ds(block * CAP, CAP)]
     mine = pl.ds(pl.multiple_of(core * share, share), share)
     other = pl.ds(pl.multiple_of((1 - core) * share, share), share)
     lanes_mine = pl.ds(pl.multiple_of(core * (depth // 2), depth // 2), depth // 2)
@@ -190,9 +231,19 @@
     w_out[x, y, :, lanes_mine] = wout_ref[mine].astype(BF16)
     w_stage[0] = win_ref[other].astype(BF16)
     w_stage[1] = wout_ref[other].astype(BF16)
+    @pl.when(at_first)
+    def _():
+        zr[...] = jnp.zeros_like(zr)
+        own_r[...] = jnp.zeros_like(own_r)
+
+    @pl.when(at_last)
+    def _():
+        zl[...] = jnp.zeros_like(zl)
+        own_l[...] = jnp.zeros_like(own_l)
+
     slots[BLOCKS * CAP:] = jnp.zeros((slots.shape[0] - BLOCKS * CAP, tiles, LANES), BF16)
 
-    pl.semaphore_wait(barrier, len(partners))
+    pl.semaphore_wait(barrier, greetings)
 
     def halves(count):
         return pl.ds(0, count // 2), pl.ds(count // 2, count // 2)
@@ -260,51 +311,119 @@
                 out["d2"] = copies.start(a_sum.at[at, low], a_r2.at[1], down)
         return out
 
+    part = CAP // 2
+
+    def chunk(j):
+        return (block + BLOCKS + j) % BLOCKS
+
     def z_begin(packed, rows):
-        at = pl.ds(block * CAP, CAP)
-        spread = {0: [copies.start(packed.at[at], rows.at[core, pl.ds(own, CAP)], line(r)) for r in range(1, LINE)]}
-        far = {}
-        for j in (1, 3, 2):
-            to = (block + j) % BLOCKS
-            far[j] = copies.start(packed.at[pl.ds(to * CAP, CAP)], rows.at[core, pl.ds(own, CAP)], twin(j))
-        return spread, far
-
-    def chunk(j):
-        return (block + BLOCKS - j) % BLOCKS
-
-    def z_relay(state, rows, j):
-        spread, far = state
-        far[j].wait_recv()
-        at = pl.ds(row_at(chunk(j), place), CAP)
-        spread[j] = [copies.start(rows.at[core, at], rows.at[core, at], line(r)) for r in range(1, LINE)]
-
-    def z_share(state, rows, j):
-        arrive(*state[0][j])
-        at = pl.ds(row_at(chunk(j), 0), rows_b)
-        return copies.start(rows.at[core, at], rows.at[core, at], mate)
+        here = pl.ds(row_at(block, place), CAP)
+        mine_at = pl.ds(block * CAP, CAP)
+        state = {"rows": rows, "edge": {}, "relay": {}}
+        state["r1"] = copies.start(packed.at[mine_at], rows.at[core, here], front, not_last)
+        state["l1"] = copies.start(packed.at[mine_at], rows.at[core, here], back_z, not_first)
+        for step in (1, 2):
+            for sign in (1, -1):
+                to = chunk(sign * step)
+                skip = part if (step == 2 and sign == -1) else 0
+                count = CAP if step == 1 else part
+                first = copies.slots(LINE)
+                src = packed.at[pl.ds(to * CAP + skip, count)]
+                dst = rows.at[core, pl.ds(row_at(block, place) + skip, count)]
+                copies.start(src, dst, seat(sign * step, 0 if sign == 1 else last), recv=first + place)
+                state["edge"][sign * step] = (first, skip, count)
+        return state
+
+    def z_line(state, n):
+        rows = state["rows"]
+        for key, sign, ahead, came, go in (("r", 1, front, place >= n, not_last), ("l", -1, back_z, place + n <= last, not_first)):
+            state[key + str(n)].wait_recv(came)
+            if n < last:
+                at = pl.ds(row_at(block, jnp.clip(place - sign * n, 0, last)), CAP)
+                state[key + str(n + 1)] = copies.start(rows.at[core, at], rows.at[core, at], ahead, came & go)
+
+    def z_edge(state, step):
+        rows = state["rows"]
+        for i in range(LINE):
+            for sign, ahead, entry, inner, go in (
+                (1, front, at_first, not_first, not_last), (-1, back_z, at_last, not_last, not_first),
+            ):
+                first, skip, count = state["edge"][sign * step]
+                source = last - i if sign == 1 else i
+                at = rows.at[core, pl.ds(row_at(chunk(-sign * step), source) + skip, count)]
+                direct = copies.make(at, at, mate, recv=first + source, send=0)
+                guarded(entry, direct.wait_recv)
+                key = (sign * step, source)
+                relay = copies.start(at, at, ahead, go & entry)
+                state["relay"][key] = relay
+                relay.wait_recv(inner)
+                inside = Copy(relay.copy, go & inner)
+                guarded(inside.when, inside.copy.start)
+                copies.started.append(inside)
+
+    def z_share(state, j):
+        at = state["rows"].at[core, pl.ds(row_at(chunk(j), 0), rows_b)]
+        return copies.start(at, at, mate)
 
     def back_share(j):
         at = pl.ds(row_at(chunk(j), 0), rows_b)
-        return {"m": copies.start(p3.at[1 - core, at], p_mate.at[at], mate)}
-
-    def back_line(out, j):
+        return copies.start(p3.at[1 - core, at], p_mate.at[at], mate)
+
+    def back_sum(copy, j):
         at = pl.ds(row_at(chunk(j), 0), rows_b)
-        out["m"].wait_recv()
-        q3[j] = add16(p3[core, at], p_mate[at])
-        out["z"] = []
-        for r in range(1, LINE):
-            to = ((place + r) % LINE) * CAP
-            out["z"].append(copies.start(q3.at[j, pl.ds(to, CAP)], rl.at[j, r - 1], line(r)))
-
-    def back_far(out, j):
-        arrive(*out["z"])
-        total = add16(q3[j, pl.ds(place * CAP, CAP)], rl[j, 0], rl[j, 1], rl[j, 2])
-        at = pl.ds(block * CAP, CAP)
-        if j == 0:
-            slots[at] = total
-        else:
-            sb[j - 1] = total
-            out["far"] = copies.start(sb.at[j - 1], slots.at[at], twin(BLOCKS - j))
+        copy.wait_recv()
+        q3[at] = add16(p3[core, at], p_mate[at])
+
+    def back_chain(step):
+        ends = []
+        for sign in (1, -1):
+            ends.append(copies.slots(1))
+        for i in range(LINE):
+            for sign, ahead, inner, go, leave, buf, out in (
+                (1, front, not_first, not_last, at_last, zr, zs_r), (-1, back_z, not_last, not_first, at_first, zl, zs_l),
+            ):
+                skip = part if (step == 2 and sign == -1) else 0
+                count = CAP if step == 1 else part
+                source = last - i if sign == 1 else i
+                slot = (step - 1) * LINE + source
+                src = out.at[slot, pl.ds(0, count)]
+                relay = copies.make(src, buf.at[slot, pl.ds(0, count)], ahead)
+                guarded(inner, relay.wait_recv)
+                at = pl.ds(row_at(chunk(sign * step), source) + skip, count)
+                out[slot, 0:count] = add16(q3[at], buf[slot, 0:count])
+                kept = Copy(relay, go)
+                guarded(go, relay.start)
+                copies.started.append(kept)
+                end = ends[0 if sign == 1 else 1]
+                copies.start(
+                    src, slots.at[pl.ds(block * CAP + skip, count)], seat(sign * step, source), leave, recv=end
+                )
+        waits = []
+        for sign, end in ((1, ends[0]), (-1, ends[1])):
+            skip = part if (step == 2 and sign == -1) else 0
+            count = CAP if step == 1 else part
+            at = slots.at[pl.ds(chunk(-sign * step) * CAP + skip, count)]
+            waits.append(copies.make(at, at, mate, recv=end, send=0))
+        return waits
+
+    def back_own():
+        for n in (3, 2, 1):
+            for key, sign, ahead, buf, out in (("r", 1, front, own_r, own_sr), ("l", -1, back_z, own_l, own_sl)):
+                target = place + sign * n
+                valid = (target >= 0) & (target <= last)
+                at = pl.ds(row_at(block, jnp.clip(target, 0, last)), CAP)
+                behind = (place - sign >= 0) & (place - sign <= last)
+                if n < last:
+                    own_state[key + str(n + 1)].wait_recv(valid & behind)
+                out[n - 1] = add16(q3[at], buf[n])
+                own_state[key + str(n)] = copies.start(out.at[n - 1], buf.at[n - 1], ahead, valid)
+
+    def back_own_end():
+        own_state["r1"].wait_recv(not_first)
+        own_state["l1"].wait_recv(not_last)
+        slots[pl.ds(block * CAP, CAP)] = add16(q3[pl.ds(row_at(block, place), CAP)], own_r[0], own_l[0])
+
+    own_state = {}
 
     def in_x(i):
         return w_in.at[y, i]
@@ -318,123 +437,146 @@
     def out_x(s):
         return lambda i: w_out.at[i, s]
 
+    def forward(i):
+        pre = None
+        for k in range(NY):
+            term = lax.dot_general(
+                x2[k], w_in[k, i], (((1,), (1,)), ((), ())), preferred_element_type=F32
+            )
+            pre = term if pre is None else pre + term
+        pre = pre * scale_in
+        square = pre * pre
+        tangent = jnp.tanh(gelu_coef * (pre + cubic_coef * square * pre))
+        hid[i] = (0.5 * pre * (1.0 + tangent)).astype(BF16).T
+        pre_slope[i] = scale_out * (
+            0.5 * (1.0 + tangent) + 0.5 * pre * (1.0 - tangent * tangent) * gelu_coef * (1.0 + 3.0 * cubic_coef * square)
+        )
+
+    def out_grads(i):
+        for k in range(NY):
+            d_out[i, k] = (jnp.dot(hid[i], g2[k], preferred_element_type=F32) * scale_out).astype(BF16)
+
+    def hidden_grads(k, begin):
+        for i in range(NX):
+            term = lax.dot_general(
+                g2[k], w_out[i, k], (((1,), (1,)), ((), ())), preferred_element_type=F32
+            )
+            grad_sum[i] = term if begin else grad_sum[i] + term
+
+    def in_grads(k):
+        for i in range(NX):
+            d_in[k, i] = (jnp.dot(pg_t[i], x2[k], preferred_element_type=F32) * scale_in).astype(BF16)
+
+    order = (0, 1, 3, 2)
     w_pair = [
         copies.start(w_stage.at[0], w_in.at[y, x, :, lanes_mine], mate),
         copies.start(w_stage.at[1], w_out.at[x, y, :, lanes_mine], mate),
     ]
+    t_state = z_begin(pk_t, x3)
     attn_sent = {}
     for q in (2, 1, 3, 0):
         at = (y + q) % NY
         attn_sent[q] = copies.start(attn_ref.at[at, 1 - core], a_mate.at[at], mate)
-    t_state = z_begin(pk_t, x3)
     arrive(w_pair[0])
     in_first = gather_first(in_x, X_RING)
+    arrive(w_pair[1])
     attn_ring = attn_begin(attn_sent)
-    arrive(w_pair[1])
     out_first = gather_first(out_y, Y_RING)
     in_big, out_big = {}, {}
     in_big[0] = gather_first(in_y(x), Y_RING)
     out_big[0] = gather_first(out_x(y), X_RING)
-    z_relay(t_state, x3, 1)
+    z_line(t_state, 1)
     in_next = gather_next(in_first, in_x, X_RING)
+    z_edge(t_state, 1)
     for q in (1, 3):
         in_big[q] = gather_first(in_y((x + q) % NX), Y_RING)
-    z_relay(t_state, x3, 3)
-    a_low, a_high = halves(n_tok)
+    z_line(t_state, 2)
     scatter_middle(attn_ring, lambda i: a_sum.at[i], n_tok, a_r1, a_m3, a_r3, Y_RING)
     out_next = gather_next(out_first, out_y, Y_RING)
     for q in (1, 3):
         out_big[q] = gather_first(out_x((y + q) % NY), X_RING)
-    z_relay(t_state, x3, 2)
+    z_edge(t_state, 2)
     arrive(*in_next)
     in_big[2] = gather_first(in_y((x + 2) % NX), Y_RING)
-    t_share = {0: z_share(t_state, x3, 0), 1: z_share(t_state, x3, 1)}
+    z_line(t_state, 3)
     first, second = scatter_end(attn_ring, lambda i: a_sum.at[i], n_tok, a_r2, a_r3, Y_RING)
     summed = jnp.concatenate([first, second], axis=0)
     pack((gate_col * summed).astype(BF16), pk_g)
-    g3[core, pl.ds(own, CAP)] = pk_g[pl.ds(block * CAP, CAP)]
+    g3[core, pl.ds(row_at(block, place), CAP)] = pk_g[pl.ds(block * CAP, CAP)]
     g_state = z_begin(pk_g, g3)
+    t_share = [z_share(t_state, j) for j in range(4)]
+    arrive(*out_next)
+    out_big[2] = gather_first(out_x((y + 2) % NY), X_RING)
     in_last, out_last = {}, {}
     in_last[0] = gather_next(in_big[0], in_y(x), Y_RING)
-    arrive(*out_next)
-    out_big[2] = gather_first(out_x((y + 2) % NY), X_RING)
     out_last[0] = gather_next(out_big[0], out_x(y), X_RING)
-    t_share[3] = z_share(t_state, x3, 3)
-    t_share[2] = z_share(t_state, x3, 2)
+    to_wide(x3, x2, core)
+    z_line(g_state, 1)
+    z_edge(g_state, 1)
+    arrive(*t_share)
+    to_wide(x3, x2, 1 - core)
+    z_line(g_state, 2)
     for q in (1, 3):
         in_last[q] = gather_next(in_big[q], in_y((x + q) % NX), Y_RING)
         out_last[q] = gather_next(out_big[q], out_x((y + q) % NY), X_RING)
-        z_relay(g_state, g3, q)
+    arrive(*in_last[0])
+    forward(x)
+    z_edge(g_state, 2)
+    z_line(g_state, 3)
+    g_share = [z_share(g_state, j) for j in range(4)]
+    to_wide(g3, g2, core)
     in_last[2] = gather_next(in_big[2], in_y((x + 2) % NX), Y_RING)
     out_last[2] = gather_next(out_big[2], out_x((y + 2) % NY), X_RING)
-    z_relay(g_state, g3, 2)
-    g_share = {}
-    g_share[0] = z_share(g_state, g3, 0)
-
-    to_wide(x3, x2, core)
-    arrive(*t_share.values())
-    to_wide(x3, x2, 1 - core)
-    for q in range(4):
+    arrive(*g_share)
+    to_wide(g3, g2, 1 - core)
+    out_grads(x)
+    arrive(*out_last[0])
+    hidden_grads(y, True)
+    for q in (1, 3):
         arrive(*in_last[q])
-    pre = None
-    for k in range(NY):
-        term = lax.dot_general(
-            x2[k], w_in[k].reshape(units, depth), (((1,), (1,)), ((), ())), preferred_element_type=F32
-        )
-        pre = term if pre is None else pre + term
-    pre = pre * scale_in
-    square = pre * pre
-    tangent = jnp.tanh(gelu_coef * (pre + cubic_coef * square * pre))
-    hid[...] = (0.5 * pre * (1.0 + tangent)).astype(BF16)
-    pre_slope[...] = scale_out * (
-        0.5 * (1.0 + tangent) + 0.5 * pre * (1.0 - tangent * tangent) * gelu_coef * (1.0 + 3.0 * cubic_coef * square)
-    )
-    for q in (1, 3, 2):
-        g_share[q] = z_share(g_state, g3, q)
-    hid_t = hid[...].T
-    to_wide(g3, g2, core)
-    arrive(*g_share.values())
-    to_wide(g3, g2, 1 - core)
-
-    for k in range(NY):
-        grads = (jnp.dot(hid_t, g2[k], preferred_element_type=F32) * scale_out).astype(BF16)
-        for i in range(NX):
-            d_out[i, k] = grads[i * share:(i + 1) * share]
+        forward((x + q) % NX)
+        out_grads((x + q) % NX)
+        arrive(*out_last[q])
+        hidden_grads((y + q) % NY, False)
+    arrive(*in_last[2])
+    forward((x + 2) % NX)
+    out_grads((x + 2) % NX)
     out_ring = scatter_first(lambda i: d_out.at[i], NY, o_r1, o_r2, X_RING)
-
-    for q in range(4):
-        arrive(*out_last[q])
-    total = None
-    for k in range(NY):
-        columns = jnp.concatenate([w_out[i, k] for i in range(NX)], axis=0)
-        term = lax.dot_general(g2[k], columns, (((1,), (1,)), ((), ())), preferred_element_type=F32)
-        total = term if total is None else total + term
-    pg[...] = (total * pre_slope[...]).astype(BF16)
+    arrive(*out_last[2])
+    hidden_grads((y + 2) % NY, False)
+    for i in range(NX):
+        grad = (grad_sum[i] * pre_slope[i]).astype(BF16)
+        pg[i] = grad
+        pg_t[i] = grad.T
+    for q in (2, 1, 3):
+        in_grads((y + q) % NY)
+    in_ring = scatter_first(lambda i: d_in.at[i], NX, i_r1, i_r2, Y_RING)
 
     back = {}
-    order = (0, 1, 3, 2)
-    for part in range(2):
-        half = (1 - core) if part == 0 else core
-        rows = pg[pl.ds(pl.multiple_of(half * rows_d, rows_d), rows_d)]
+    for part_i in range(2):
+        half = (1 - core) if part_i == 0 else core
         for k in range(NY):
-            p2[k] = (
-                jnp.dot(rows, w_in[k].reshape(units, depth), preferred_element_type=F32) * scale_in
-            ).astype(BF16)
+            term = None
+            for i in range(NX):
+                add = jnp.dot(
+                    pg[i, pl.ds(pl.multiple_of(half * rows_d, rows_d), rows_d)], w_in[k, i],
+                    preferred_element_type=F32,
+                )
+                term = add if term is None else term + add
+            p2[k] = (term * scale_in).astype(BF16)
         to_narrow(p2, p3, half)
-        if part == 0:
+        if part_i == 0:
             for j in order:
                 back[j] = back_share(j)
-    scatter_middle(out_ring, lambda i: d_out.at[i], NY, o_r1, o_m3, o_r3, X_RING)
+            scatter_middle(out_ring, lambda i: d_out.at[i], NY, o_r1, o_m3, o_r3, X_RING)
     for j in order:
-        back_line(back[j], j)
-    pg_t = pg[...].T
-    for k in range(NY):
-        grads = (jnp.dot(pg_t, x2[k], preferred_element_type=F32) * scale_in).astype(BF16)
-        d_in[k] = grads.reshape(NX, share, depth)
-    in_ring = scatter_first(lambda i: d_in.at[i], NX, i_r1, i_r2, Y_RING)
-    for j in order:
-        back_far(back[j], j)
+        back_sum(back[j], j)
+    back_own()
+    ends = back_chain(1)
+    in_grads(y)
     scatter_middle(in_ring, lambda i: d_in.at[i], NX, i_r1, i_m3, i_r3, Y_RING)
+    ends += back_chain(2)
+    back_own_end()
 
     first, second = scatter_end(out_ring, lambda i: d_out.at[i], NY, o_r2, o_r3, X_RING)
     o_sum[0:2] = first.astype(BF16)
@@ -456,7 +598,8 @@
         d_part[t, high] = second.astype(BF16)
         pair.append(copies.start(d_part.at[t, :, lanes_other], d_other.at[t], mate))
 
-    arrive(back[1]["far"], back[3]["far"], back[2]["far"])
+    for copy in ends:
+        copy.wait_recv()
     wide = []
     for g in range(n_slot // 16):
         moved = jnp.dot(
@@ -483,7 +626,6 @@
     rows_b = LINE * CAP
     rows_d = BLOCKS * rows_b
     share = hidden // 2
-    units = NX * share
     depth = width // NY
     slot_rows = 48
     vmem = pl.BlockSpec(memory_space=pltpu.VMEM)
@@ -499,9 +641,11 @@
         bf16(NY, 2 * rows_d, depth), bf16(NY, 2 * rows_d, depth),
         bf16(256, 256), bf16(slot_rows, n_tok),
         bf16(2, share, depth // 2), bf16(NY, NX, share, depth), bf16(NX, NY, share, depth),
-        pltpu.VMEM((2 * rows_d, units), F32), bf16(2 * rows_d, units), bf16(2 * rows_d, units),
+        pltpu.VMEM((NX, 2 * rows_d, share), F32), pltpu.VMEM((NX, 2 * rows_d, share), F32),
+        bf16(NX, 2 * rows_d, share), bf16(NX, share, 2 * rows_d), bf16(NX, share, 2 * rows_d),
         bf16(NY, rows_d, depth), rows16(2, rows_d), rows16(rows_d),
-        rows16(BLOCKS, rows_b), rows16(BLOCKS, LINE - 1, CAP), rows16(BLOCKS - 1, CAP), rows16(slot_rows),
+        rows16(rows_d), rows16(2 * LINE, CAP), rows16(2 * LINE, CAP), rows16(2 * LINE, CAP), rows16(2 * LINE, CAP),
+        rows16(LINE, CAP), rows16(LINE, CAP), rows16(LINE, CAP), rows16(LINE, CAP), rows16(slot_rows),
         bf16(NY, n_tok, width), bf16(NY, n_tok, width),
     ]
     scratch += [bf16(2, n_tok // 2, width)] * 4

time: 129 us -> 498 us (3.86)
  Pallas kernels: 123 us -> 492 us
    pallas_call x1, Pallas kernels: 123 us -> 492 us  [shards(): pl.pallas_call(functools.partial(kernel, (width, hidden)), out_shape=(jax...]
where the time goes in v3:
time: 498 us
  Pallas kernels  492 us (99%)
  local copies, waits for them, and re-layouts  5.1 us (1%)
    pallas_call x1, Pallas kernels, shards(): pl.pallas_call(functools.partial(kernel, (width, hidden)), out_shape=(jax...  492 us

profile of v3, /device:TPU:1, one launch (start us, length us, event | category | flops | bytes accessed | tf_op | source)
XLA Modules:
  0.0 497.5 jit_solution(14448841077746004273)
XLA Ops:
  0.6 491.8 %shard_map.85 = (bf16[64,2048]{1,0:T(8,128)(2,1)}, f32[320,256]{1,0:T(8,128)}, f32[320,256]{1,0:T(8,128)}) custom-call(bf16[64,2048]{1,0:T(8,128)(2,1)} %tok_ref.1, bf16[4,2,64,2048]{3,2,1,0:T(8,128)(2,1)} %bitcast.7, s32[1,64]{1,0:T(1,128)} %bitcast.12, f32[1,64]{1,0:T(1,128)} %bitcast.13, f32[320,256]{1,0:T(8,128)} %bitcast.10, f32[320,256]{1,0:T(8,128)} %bitcast.11), custom_call_target="tpu_custom_call" | custom-call | tf_op jit(solution)/shard_map/pallas_call | solution.py:657
  492.4 1.7 copy.12
  494.1 1.7 copy.13
  495.8 1.7 copy.14

commit v4 on v3

--- a/solution.py
+++ b/solution.py
@@ -56,6 +56,11 @@
     def slots(self, count):
         first = self.recvs
         self.recvs += count
+        return first
+
+    def send_slots(self, count):
+        first = self.sends
+        self.sends += count
         return first
 
     def make(self, src, dst, device, recv=None, send=None):
@@ -85,6 +90,8 @@
 
 
 N_COPIES = 384
+CHAIN = 3
+LAG = 2
 
 
 def kernel(
@@ -311,8 +318,6 @@
                 out["d2"] = copies.start(a_sum.at[at, low], a_r2.at[1], down)
         return out
 
-    part = CAP // 2
-
     def chunk(j):
         return (block + BLOCKS + j) % BLOCKS
 
@@ -324,14 +329,15 @@
         state["l1"] = copies.start(packed.at[mine_at], rows.at[core, here], back_z, not_first)
         for step in (1, 2):
             for sign in (1, -1):
-                to = chunk(sign * step)
-                skip = part if (step == 2 and sign == -1) else 0
-                count = CAP if step == 1 else part
                 first = copies.slots(LINE)
-                src = packed.at[pl.ds(to * CAP + skip, count)]
-                dst = rows.at[core, pl.ds(row_at(block, place) + skip, count)]
-                copies.start(src, dst, seat(sign * step, 0 if sign == 1 else last), recv=first + place)
-                state["edge"][sign * step] = (first, skip, count)
+                sends = None if step == 1 else (place >= 2 if sign == 1 else place < 2)
+                copies.start(
+                    packed.at[pl.ds(chunk(sign * step) * CAP, CAP)], rows.at[core, here],
+                    seat(sign * step, 0 if sign == 1 else last), sends, recv=first + place,
+                )
+                state["edge"][sign * step] = first
+        for sign in (1, -1):
+            state["relay"][sign] = (copies.slots(CHAIN), copies.send_slots(CHAIN))
         return state
 
     def z_line(state, n):
@@ -342,24 +348,50 @@
                 at = pl.ds(row_at(block, jnp.clip(place - sign * n, 0, last)), CAP)
                 state[key + str(n + 1)] = copies.start(rows.at[core, at], rows.at[core, at], ahead, came & go)
 
-    def z_edge(state, step):
+    directions = (
+        (1, front, at_first, not_first, not_last, place), (-1, back_z, at_last, not_last, not_first, last - place),
+    )
+
+    def pair_place(sign, k):
+        return 2 * (1 - k % 2) if sign == 1 else 2 * (k % 2)
+
+    def z_chain(state, *times):
         rows = state["rows"]
-        for i in range(LINE):
-            for sign, ahead, entry, inner, go in (
-                (1, front, at_first, not_first, not_last), (-1, back_z, at_last, not_last, not_first),
-            ):
-                first, skip, count = state["edge"][sign * step]
-                source = last - i if sign == 1 else i
-                at = rows.at[core, pl.ds(row_at(chunk(-sign * step), source) + skip, count)]
-                direct = copies.make(at, at, mate, recv=first + source, send=0)
-                guarded(entry, direct.wait_recv)
-                key = (sign * step, source)
-                relay = copies.start(at, at, ahead, go & entry)
-                state["relay"][key] = relay
-                relay.wait_recv(inner)
-                inside = Copy(relay.copy, go & inner)
-                guarded(inside.when, inside.copy.start)
-                copies.started.append(inside)
+
+        def view(sign, k):
+            from_block = (block + BLOCKS - sign * (1 + k // 2)) % BLOCKS
+            return rows.at[core, pl.ds(row_at(from_block, pair_place(sign, k)), 2 * CAP)]
+
+        for t in times:
+            for sign, ahead, entry, inner, go, rank in directions:
+                recv, send = state["relay"][sign]
+                if t < CHAIN:
+                    at = view(sign, t)
+                    first = state["edge"][sign * (1 + t // 2)] + pair_place(sign, t)
+                    start = copies.make(at, at, ahead, recv + t, send + t)
+                    half_at = rows.at[core, pl.ds(row_at(0, 0), CAP)]
+                    arrivals = [copies.make(half_at, half_at, mate, first + n, 0) for n in range(2)]
+
+                    def enter(start=start, arrivals=arrivals):
+                        for copy in arrivals:
+                            copy.wait_recv()
+                        start.start()
+
+                    pl.when(entry)(enter)
+                k = t - LAG * rank
+                safe = jnp.clip(k, 0, CHAIN - 1)
+                at = view(sign, safe)
+                relay = copies.make(at, at, ahead, recv + safe, send + safe)
+
+                def pass_on(relay=relay, go=go):
+                    relay.wait_recv()
+                    pl.when(go)(relay.start)
+
+                pl.when(inner & (k >= 0) & (k < CHAIN))(pass_on)
+                if t == CHAIN - 1 + LAG * last:
+                    for n in range(CHAIN):
+                        sent = copies.make(view(sign, n), view(sign, n), ahead, recv + n, send + n)
+                        copies.started.append(Copy(sent, go))
 
     def z_share(state, j):
         at = state["rows"].at[core, pl.ds(row_at(chunk(j), 0), rows_b)]
@@ -374,37 +406,56 @@
         copy.wait_recv()
         q3[at] = add16(p3[core, at], p_mate[at])
 
-    def back_chain(step):
-        ends = []
+    def back_chain(state, *times):
+        if not state:
+            for sign in (1, -1):
+                state[sign] = (copies.slots(CHAIN), copies.send_slots(CHAIN), copies.slots(2), copies.send_slots(2 * CHAIN))
+        for t in times:
+            for (sign, ahead, entry, inner, go, rank), buf, out in zip(directions, (zr, zl), (zs_r, zs_l)):
+                recv, send, end, send_end = state[sign]
+                k = t - LAG * rank
+                safe = jnp.clip(k, 0, CHAIN - 1)
+                step = 1 + safe // 2
+                to_block = (block + BLOCKS + sign * step) % BLOCKS
+                first = pair_place(-sign, safe)
+                relay = copies.make(out.at[safe], buf.at[safe], ahead, recv + safe, send + safe)
+                leaving = [
+                    copies.make(
+                        out.at[safe, pl.ds(n * CAP, CAP)], slots.at[pl.ds(block * CAP, CAP)],
+                        ((to_block * LINE + first + n) * NX + x, dp), end + safe // 2, send_end + 2 * safe + n,
+                    )
+                    for n in range(2)
+                ]
+
+                def pass_on(
+                    relay=relay, leaving=leaving, inner=inner, go=go, buf=buf, out=out, safe=safe,
+                    at=pl.ds(row_at(to_block, first), 2 * CAP),
+                ):
+                    pl.when(inner)(relay.wait_recv)
+                    out[safe] = add16(q3[at], buf[safe])
+                    pl.when(go)(relay.start)
+
+                    @pl.when(jnp.logical_not(go))
+                    def _():
+                        for copy in leaving:
+                            copy.start()
+
+                pl.when((k >= 0) & (k < CHAIN))(pass_on)
+                if t == CHAIN - 1 + LAG * last:
+                    for n in range(CHAIN):
+                        sent = copies.make(out.at[n], buf.at[n], ahead, recv + n, send + n)
+                        copies.started.append(Copy(sent, go))
+                    for n in range(2 * CHAIN):
+                        at = out.at[n // 2, pl.ds(0, CAP)]
+                        sent = copies.make(at, at, ahead, end, send_end + n)
+                        copies.started.append(Copy(sent, jnp.logical_not(go)))
+
+    def back_chain_end(state):
+        at = slots.at[pl.ds(0, CAP)]
         for sign in (1, -1):
-            ends.append(copies.slots(1))
-        for i in range(LINE):
-            for sign, ahead, inner, go, leave, buf, out in (
-                (1, front, not_first, not_last, at_last, zr, zs_r), (-1, back_z, not_last, not_first, at_first, zl, zs_l),
-            ):
-                skip = part if (step == 2 and sign == -1) else 0
-                count = CAP if step == 1 else part
-                source = last - i if sign == 1 else i
-                slot = (step - 1) * LINE + source
-                src = out.at[slot, pl.ds(0, count)]
-                relay = copies.make(src, buf.at[slot, pl.ds(0, count)], ahead)
-                guarded(inner, relay.wait_recv)
-                at = pl.ds(row_at(chunk(sign * step), source) + skip, count)
-                out[slot, 0:count] = add16(q3[at], buf[slot, 0:count])
-                kept = Copy(relay, go)
-                guarded(go, relay.start)
-                copies.started.append(kept)
-                end = ends[0 if sign == 1 else 1]
-                copies.start(
-                    src, slots.at[pl.ds(block * CAP + skip, count)], seat(sign * step, source), leave, recv=end
-                )
-        waits = []
-        for sign, end in ((1, ends[0]), (-1, ends[1])):
-            skip = part if (step == 2 and sign == -1) else 0
-            count = CAP if step == 1 else part
-            at = slots.at[pl.ds(chunk(-sign * step) * CAP + skip, count)]
-            waits.append(copies.make(at, at, mate, recv=end, send=0))
-        return waits
+            end = state[sign][2]
+            for n, came in ((0, None), (1, place < 2 if sign == 1 else place >= 2)):
+                guarded(came, copies.make(at, at, mate, end + n, 0).wait_recv)
 
     def back_own():
         for n in (3, 2, 1):
@@ -477,52 +528,58 @@
     for q in (2, 1, 3, 0):
         at = (y + q) % NY
         attn_sent[q] = copies.start(attn_ref.at[at, 1 - core], a_mate.at[at], mate)
-    arrive(w_pair[0])
+    arrive(*w_pair)
     in_first = gather_first(in_x, X_RING)
-    arrive(w_pair[1])
+    in_big, out_big, in_last, out_last = {}, {}, {}, {}
+    out_big[0] = gather_first(out_x(y), X_RING)
     attn_ring = attn_begin(attn_sent)
+    z_line(t_state, 1)
+    z_chain(t_state, 0, 1)
+    scatter_middle(attn_ring, lambda i: a_sum.at[i], n_tok, a_r1, a_m3, a_r3, Y_RING)
+    in_big[0] = gather_first(in_y(x), Y_RING)
     out_first = gather_first(out_y, Y_RING)
-    in_big, out_big = {}, {}
-    in_big[0] = gather_first(in_y(x), Y_RING)
-    out_big[0] = gather_first(out_x(y), X_RING)
-    z_line(t_state, 1)
+    z_chain(t_state, 2, 3)
+    z_line(t_state, 2)
     in_next = gather_next(in_first, in_x, X_RING)
-    z_edge(t_state, 1)
     for q in (1, 3):
         in_big[q] = gather_first(in_y((x + q) % NX), Y_RING)
-    z_line(t_state, 2)
-    scatter_middle(attn_ring, lambda i: a_sum.at[i], n_tok, a_r1, a_m3, a_r3, Y_RING)
-    out_next = gather_next(out_first, out_y, Y_RING)
-    for q in (1, 3):
-        out_big[q] = gather_first(out_x((y + q) % NY), X_RING)
-    z_edge(t_state, 2)
-    arrive(*in_next)
-    in_big[2] = gather_first(in_y((x + 2) % NX), Y_RING)
-    z_line(t_state, 3)
+    z_chain(t_state, 4, 5)
     first, second = scatter_end(attn_ring, lambda i: a_sum.at[i], n_tok, a_r2, a_r3, Y_RING)
     summed = jnp.concatenate([first, second], axis=0)
     pack((gate_col * summed).astype(BF16), pk_g)
     g3[core, pl.ds(row_at(block, place), CAP)] = pk_g[pl.ds(block * CAP, CAP)]
     g_state = z_begin(pk_g, g3)
+    z_line(t_state, 3)
+    z_chain(t_state, 6, 7)
+    arrive(*in_next)
+    in_big[2] = gather_first(in_y((x + 2) % NX), Y_RING)
+    out_next = gather_next(out_first, out_y, Y_RING)
+    for q in (1, 3):
+        out_big[q] = gather_first(out_x((y + q) % NY), X_RING)
+    z_chain(t_state, 8)
     t_share = [z_share(t_state, j) for j in range(4)]
+    z_line(g_state, 1)
+    z_chain(g_state, 0, 1)
+    to_wide(x3, x2, core)
+    in_last[0] = gather_next(in_big[0], in_y(x), Y_RING)
+    out_last[0] = gather_next(out_big[0], out_x(y), X_RING)
+    z_chain(g_state, 2)
+    z_line(g_state, 2)
+    arrive(*t_share)
+    to_wide(x3, x2, 1 - core)
+    z_chain(g_state, 3, 4)
     arrive(*out_next)
     out_big[2] = gather_first(out_x((y + 2) % NY), X_RING)
-    in_last, out_last = {}, {}
-    in_last[0] = gather_next(in_big[0], in_y(x), Y_RING)
-    out_last[0] = gather_next(out_big[0], out_x(y), X_RING)
-    to_wide(x3, x2, core)
-    z_line(g_state, 1)
-    z_edge(g_state, 1)
-    arrive(*t_share)
-    to_wide(x3, x2, 1 - core)
-    z_line(g_state, 2)
-    for q in (1, 3):
-        in_last[q] = gather_next(in_big[q], in_y((x + q) % NX), Y_RING)
-        out_last[q] = gather_next(out_big[q], out_x((y + q) % NY), X_RING)
+    in_last[1] = gather_next(in_big[1], in_y((x + 1) % NX), Y_RING)
+    in_last[3] = gather_next(in_big[3], in_y((x + 3) % NX), Y_RING)
+    z_chain(g_state, 5)
+    z_line(g_state, 3)
     arrive(*in_last[0])
     forward(x)
-    z_edge(g_state, 2)
-    z_line(g_state, 3)
+    z_chain(g_state, 6, 7)
+    out_last[1] = gather_next(out_big[1], out_x((y + 1) % NY), X_RING)
+    out_last[3] = gather_next(out_big[3], out_x((y + 3) % NY), X_RING)
+    z_chain(g_state, 8)
     g_share = [z_share(g_state, j) for j in range(4)]
     to_wide(g3, g2, core)
     in_last[2] = gather_next(in_big[2], in_y((x + 2) % NX), Y_RING)
@@ -571,11 +628,14 @@
             scatter_middle(out_ring, lambda i: d_out.at[i], NY, o_r1, o_m3, o_r3, X_RING)
     for j in order:
         back_sum(back[j], j)
+    ends = {}
+    back_chain(ends, 0)
     back_own()
-    ends = back_chain(1)
+    back_chain(ends, 1, 2)
     in_grads(y)
+    back_chain(ends, 3, 4)
     scatter_middle(in_ring, lambda i: d_in.at[i], NX, i_r1, i_m3, i_r3, Y_RING)
-    ends += back_chain(2)
+    back_chain(ends, 5, 6, 7, 8)
     back_own_end()
 
     first, second = scatter_end(out_ring, lambda i: d_out.at[i], NY, o_r2, o_r3, X_RING)
@@ -598,8 +658,7 @@
         d_part[t, high] = second.astype(BF16)
         pair.append(copies.start(d_part.at[t, :, lanes_other], d_other.at[t], mate))
 
-    for copy in ends:
-        copy.wait_recv()
+    back_chain_end(ends)
     wide = []
     for g in range(n_slot // 16):
         moved = jnp.dot(
@@ -644,7 +703,7 @@
         pltpu.VMEM((NX, 2 * rows_d, share), F32), pltpu.VMEM((NX, 2 * rows_d, share), F32),
         bf16(NX, 2 * rows_d, share), bf16(NX, share, 2 * rows_d), bf16(NX, share, 2 * rows_d),
         bf16(NY, rows_d, depth), rows16(2, rows_d), rows16(rows_d),
-        rows16(rows_d), rows16(2 * LINE, CAP), rows16(2 * LINE, CAP), rows16(2 * LINE, CAP), rows16(2 * LINE, CAP),
+        rows16(rows_d), rows16(CHAIN, 2 * CAP), rows16(CHAIN, 2 * CAP), rows16(CHAIN, 2 * CAP), rows16(CHAIN, 2 * CAP),
         rows16(LINE, CAP), rows16(LINE, CAP), rows16(LINE, CAP), rows16(LINE, CAP), rows16(slot_rows),
         bf16(NY, n_tok, width), bf16(NY, n_tok, width),
     ]

time: 498 us -> 124 us (0.25)
  Pallas kernels: 492 us -> 117 us
    pallas_call x1, Pallas kernels: 492 us -> 117 us  [shards(): pl.pallas_call(functools.partial(kernel, (width, hidden)), out_shape=(jax...]
where the time goes in v4:
time: 124 us; the launch traced here: 123 us
  Pallas kernels  117 us (94%)
  local copies, waits for them, and re-layouts  5.1 us (4%)
    pallas_call x1, Pallas kernels, shards(): pl.pallas_call(functools.partial(kernel, (width, hidden)), out_shape=(jax...  117 us
    unnamed x3, local copies, waits for them, and re-layouts  5.1 us

profile of v4, /device:TPU:1, one launch (start us, length us, event | category | flops | bytes accessed | tf_op | source)
XLA Modules:
  0.0 122.7 jit_solution(9870317700727316512)
XLA Ops:
  0.6 116.9 %shard_map.85 = (bf16[64,2048]{1,0:T(8,128)(2,1)}, f32[320,256]{1,0:T(8,128)}, f32[320,256]{1,0:T(8,128)}) custom-call(bf16[64,2048]{1,0:T(8,128)(2,1)} %tok_ref.1, bf16[4,2,64,2048]{3,2,1,0:T(8,128)(2,1)} %bitcast.7, s32[1,64]{1,0:T(1,128)} %bitcast.12, f32[1,64]{1,0:T(1,128)} %bitcast.13, f32[320,256]{1,0:T(8,128)} %bitcast.10, f32[320,256]{1,0:T(8,128)} %bitcast.11), custom_call_target="tpu_custom_call" | custom-call | tf_op jit(solution)/shard_map/pallas_call | solution.py:716
  117.6 1.7 %copy.12 = bf16[64,2048]{1,0:T(8,128)(2,1)} copy(bf16[64,2048]{1,0:T(8,128)(2,1)} %get-tuple-element.12) | data formatting | bytes 524288
  119.3 1.7 %copy.13 = f32[256,320]{0,1:T(8,128)} copy(f32[256,320]{0,1:T(8,128)} %bitcast.9) | data formatting | bytes 655360
  121.0 1.7 %copy.14 = f32[256,320]{0,1:T(8,128)} copy(f32[256,320]{0,1:T(8,128)} %bitcast.8) | data formatting | bytes 655360

commit v5 on v4

--- a/solution.py
+++ b/solution.py
@@ -105,7 +105,7 @@
     d_in, i_r1, i_m3, i_r3, i_r2, i_sum, is_r1, is_m3, is_r3, is_r2,
     d_out, o_r1, o_m3, o_r3, o_r2, o_sum, os_r1, os_m3, os_r3, os_r2,
     d_part, d_other,
-    send_sems, recv_sems,
+    send_sems, recv_sems, reach_sems,
 ):
     width, hidden = dims
     scale_in = width ** (-0.5)
@@ -139,23 +139,22 @@
     def seat(step, at):
         return ((((block + step + BLOCKS) % BLOCKS) * LINE + at) * NX + x, dp)
 
+    def z_step(step):
+        return ((z + step + BLOCKS * LINE) % (BLOCKS * LINE) * NX + x, dp)
+
     barrier = pltpu.get_barrier_semaphore()
-
-    def greet(device, when=None):
-        guarded(when, lambda: pl.semaphore_signal(barrier, inc=1, device_id=device, device_id_type=MESH))
-
-    for device in (right, left, up, down, mate):
-        greet(device)
-    greet(front, not_last)
-    greet(back_z, not_first)
-    for step in (1, 2):
-        greet(seat(step, 0))
-        greet(seat(-step, last))
-        for at in range(LINE):
-            greet(seat(step, at), at_last)
-            greet(seat(-step, at), at_first)
-    edge = jnp.where(at_first | at_last, 2 * LINE - 1, 0)
-    greetings = 5 + 2 + 4 + edge
+    near = (right, left, up, down, mate, front, back_z)
+    for device in near:
+        pl.semaphore_signal(barrier, inc=1, device_id=device, device_id_type=MESH)
+
+    def reach(round_index):
+        for step in ((1, -1), (2, -2), (4, -4))[round_index]:
+            pl.semaphore_signal(
+                reach_sems.at[round_index], inc=1, device_id=z_step(step), device_id_type=MESH
+            )
+
+    def reached(round_index):
+        pl.semaphore_wait(reach_sems.at[round_index], 2)
 
     copies = Copies(send_sems, recv_sems)
 
@@ -163,28 +162,10 @@
         for copy in waiting:
             copy.wait_recv()
 
-    row_i = lax.broadcasted_iota(jnp.int32, (256, 256), 0)
-    col_i = lax.broadcasted_iota(jnp.int32, (256, 256), 1)
-    perm[...] = jnp.where(col_i == (row_i % 16) * 16 + row_i // 16, 1.0, 0.0).astype(BF16)
-
     n_tok = tok_ref.shape[0]
-    ids_row = ids_ref[...].astype(F32)
-    eye_t = lax.broadcasted_iota(jnp.int32, (n_tok, n_tok), 0)
-    eye_s = lax.broadcasted_iota(jnp.int32, (n_tok, n_tok), 1)
-    spread_ids = jnp.broadcast_to(ids_row, (n_tok, n_tok))
-    ids_col = jnp.sum(jnp.where(eye_t == eye_s, spread_ids, 0.0), axis=1, keepdims=True)
-    earlier = jnp.where((ids_col == spread_ids) & (eye_t < eye_s), 1.0, 0.0)
-    rank_row = jnp.sum(earlier, axis=0, keepdims=True)
-    slot_row = jnp.where(rank_row < CAP, ids_row * CAP + rank_row, -1.0)
-    n_slot = disp.shape[0]
-    slot_i = lax.broadcasted_iota(jnp.int32, (n_slot, n_tok), 0).astype(F32)
-    disp[...] = jnp.where(slot_i == jnp.broadcast_to(slot_row, (n_slot, n_tok)), 1.0, 0.0).astype(BF16)
-    gate_col = jnp.sum(
-        jnp.where(eye_t == eye_s, jnp.broadcast_to(gate_ref[...], (n_tok, n_tok)), 0.0),
-        axis=1, keepdims=True,
-    )
 
     def pack(rows, dst):
+        n_slot = disp.shape[0]
         packed = jnp.dot(disp[...], rows, preferred_element_type=F32).astype(BF16)
         for g in range(n_slot // 16):
             stacked = jnp.concatenate(
@@ -224,12 +205,9 @@
 
         lax.fori_loop(0, rows_d // 32, body, 0)
 
-    pack(tok_ref[...], pk_t)
-
     def row_at(c, p):
         return c * rows_b + p * CAP
 
-    x3[core, pl.ds(row_at(block, place), CAP)] = pk_t[pl.ds(block * CAP, CAP)]
     mine = pl.ds(pl.multiple_of(core * share, share), share)
     other = pl.ds(pl.multiple_of((1 - core) * share, share), share)
     lanes_mine = pl.ds(pl.multiple_of(core * (depth // 2), depth // 2), depth // 2)
@@ -238,19 +216,8 @@
     w_out[x, y, :, lanes_mine] = wout_ref[mine].astype(BF16)
     w_stage[0] = win_ref[other].astype(BF16)
     w_stage[1] = wout_ref[other].astype(BF16)
-    @pl.when(at_first)
-    def _():
-        zr[...] = jnp.zeros_like(zr)
-        own_r[...] = jnp.zeros_like(own_r)
-
-    @pl.when(at_last)
-    def _():
-        zl[...] = jnp.zeros_like(zl)
-        own_l[...] = jnp.zeros_like(own_l)
-
-    slots[BLOCKS * CAP:] = jnp.zeros((slots.shape[0] - BLOCKS * CAP, tiles, LANES), BF16)
-
-    pl.semaphore_wait(barrier, greetings)
+    pl.semaphore_wait(barrier, len(near))
+    reach(0)
 
     def halves(count):
         return pl.ds(0, count // 2), pl.ds(count // 2, count // 2)
@@ -523,16 +490,55 @@
         copies.start(w_stage.at[0], w_in.at[y, x, :, lanes_mine], mate),
         copies.start(w_stage.at[1], w_out.at[x, y, :, lanes_mine], mate),
     ]
-    t_state = z_begin(pk_t, x3)
     attn_sent = {}
     for q in (2, 1, 3, 0):
         at = (y + q) % NY
         attn_sent[q] = copies.start(attn_ref.at[at, 1 - core], a_mate.at[at], mate)
+    reached(0)
+    reach(1)
+    row_i = lax.broadcasted_iota(jnp.int32, (256, 256), 0)
+    col_i = lax.broadcasted_iota(jnp.int32, (256, 256), 1)
+    perm[...] = jnp.where(col_i == (row_i % 16) * 16 + row_i // 16, 1.0, 0.0).astype(BF16)
+
+    ids_row = ids_ref[...].astype(F32)
+    eye_t = lax.broadcasted_iota(jnp.int32, (n_tok, n_tok), 0)
+    eye_s = lax.broadcasted_iota(jnp.int32, (n_tok, n_tok), 1)
+    spread_ids = jnp.broadcast_to(ids_row, (n_tok, n_tok))
+    ids_col = jnp.sum(jnp.where(eye_t == eye_s, spread_ids, 0.0), axis=1, keepdims=True)
+    earlier = jnp.where((ids_col == spread_ids) & (eye_t < eye_s), 1.0, 0.0)
+    rank_row = jnp.sum(earlier, axis=0, keepdims=True)
+    slot_row = jnp.where(rank_row < CAP, ids_row * CAP + rank_row, -1.0)
+    n_slot = disp.shape[0]
+    slot_i = lax.broadcasted_iota(jnp.int32, (n_slot, n_tok), 0).astype(F32)
+    disp[...] = jnp.where(slot_i == jnp.broadcast_to(slot_row, (n_slot, n_tok)), 1.0, 0.0).astype(BF16)
+    gate_col = jnp.sum(
+        jnp.where(eye_t == eye_s, jnp.broadcast_to(gate_ref[...], (n_tok, n_tok)), 0.0),
+        axis=1, keepdims=True,
+    )
+
+    reached(1)
+    reach(2)
     arrive(*w_pair)
     in_first = gather_first(in_x, X_RING)
     in_big, out_big, in_last, out_last = {}, {}, {}, {}
     out_big[0] = gather_first(out_x(y), X_RING)
+    pack(tok_ref[...], pk_t)
+    x3[core, pl.ds(row_at(block, place), CAP)] = pk_t[pl.ds(block * CAP, CAP)]
+    reached(2)
+    t_state = z_begin(pk_t, x3)
     attn_ring = attn_begin(attn_sent)
+    @pl.when(at_first)
+    def _():
+        zr[...] = jnp.zeros_like(zr)
+        own_r[...] = jnp.zeros_like(own_r)
+
+    @pl.when(at_last)
+    def _():
+        zl[...] = jnp.zeros_like(zl)
+        own_l[...] = jnp.zeros_like(own_l)
+
+    slots[BLOCKS * CAP:] = jnp.zeros((slots.shape[0] - BLOCKS * CAP, tiles, LANES), BF16)
+
     z_line(t_state, 1)
     z_chain(t_state, 0, 1)
     scatter_middle(attn_ring, lambda i: a_sum.at[i], n_tok, a_r1, a_m3, a_r3, Y_RING)
@@ -579,19 +585,20 @@
     z_chain(g_state, 6, 7)
     out_last[1] = gather_next(out_big[1], out_x((y + 1) % NY), X_RING)
     out_last[3] = gather_next(out_big[3], out_x((y + 3) % NY), X_RING)
+    arrive(*in_last[1], *in_last[3])
     z_chain(g_state, 8)
     g_share = [z_share(g_state, j) for j in range(4)]
-    to_wide(g3, g2, core)
     in_last[2] = gather_next(in_big[2], in_y((x + 2) % NX), Y_RING)
     out_last[2] = gather_next(out_big[2], out_x((y + 2) % NY), X_RING)
+    forward((x + 1) % NX)
+    forward((x + 3) % NX)
+    to_wide(g3, g2, core)
     arrive(*g_share)
     to_wide(g3, g2, 1 - core)
     out_grads(x)
     arrive(*out_last[0])
     hidden_grads(y, True)
     for q in (1, 3):
-        arrive(*in_last[q])
-        forward((x + q) % NX)
         out_grads((x + q) % NX)
         arrive(*out_last[q])
         hidden_grads((y + q) % NY, False)
@@ -677,6 +684,11 @@
     copies.finish()
 
 
+def hand_over(*refs):
+    for source, target in zip(refs[:3], refs[3:]):
+        target[...] = source[...]
+
+
 def shards(tokens, attn_partials, expert_ids, gate, w_in, w_out):
     n_tok, width = tokens.shape
     w_in_t, w_out_t = w_in.T, w_out.T
@@ -713,6 +725,7 @@
         scratch += [bf16(4, share, depth)] + [bf16(2, share // 2, depth)] * 4
     scratch += [bf16(2, share, depth), bf16(2, share, depth // 2)]
     scratch += [pltpu.SemaphoreType.DMA((N_COPIES,)), pltpu.SemaphoreType.DMA((N_COPIES,))]
+    scratch += [pltpu.SemaphoreType.REGULAR((3,))]
     token_grad, new_in, new_out = pl.pallas_call(
         functools.partial(kernel, (width, hidden)),
         out_shape=(
@@ -734,6 +747,13 @@
         w_in_t,
         w_out_t,
     )
+    results = (token_grad, new_in, new_out)
+    token_grad, new_in, new_out = pl.pallas_call(
+        hand_over,
+        out_shape=tuple(jax.ShapeDtypeStruct(r.shape, r.dtype) for r in results),
+        in_specs=[vmem] * 3,
+        out_specs=(vmem, vmem, vmem),
+    )(*results)
     return token_grad, new_in.T, new_out.T
 
 

time: 124 us -> 121 us (0.976)
  local copies, waits for them, and re-layouts: 5.1 us -> 0 us
  Pallas kernels: 117 us -> 120 us
    unnamed x3 -> x0, local copies, waits for them, and re-layouts: 5.1 us -> none
    pallas_call x0 -> x1, Pallas kernels: none -> 2.09 us  [shards(): pl.pallas_call(hand_over, out_shape=tuple((jax.ShapeDtypeStruct(r.shape,...]
where the time goes in v5:
time: 121 us
  Pallas kernels  120 us (99%)
    pallas_call x1, Pallas kernels, shards(): pl.pallas_call(functools.partial(kernel, (width, hidden)), out_shape=(jax...  118 us

profile of v5, /device:TPU:1, one launch (start us, length us, event | category | flops | bytes accessed | tf_op | source)
XLA Modules:
  0.0 120.7 jit_solution(14548237153292488203)
XLA Ops:
  0.6 118.0 %shard_map.85 = (bf16[64,2048]{1,0:T(8,128)(2,1)}, f32[320,256]{1,0:T(8,128)}, f32[320,256]{1,0:T(8,128)}) custom-call(bf16[64,2048]{1,0:T(8,128)(2,1)} %tok_ref.1, bf16[4,2,64,2048]{3,2,1,0:T(8,128)(2,1)} %bitcast.7, s32[1,64]{1,0:T(1,128)} %bitcast.10, f32[1,64]{1,0:T(1,128)} %bitcast.11, f32[320,256]{1,0:T(8,128)} %bitcast.8, f32[320,256]{1,0:T(8,128)} %bitcast.9), custom_call_target="tpu_custom_call" | custom-call | tf_op jit(solution)/shard_map/pallas_call | solution.py:729
  118.6 2.1 %shard_map.86 = (bf16[64,2048]{1,0:T(8,128)(2,1)}, f32[320,256]{1,0:T(8,128)}, f32[320,256]{1,0:T(8,128)}) custom-call(bf16[64,2048]{1,0:T(8,128)(2,1)} %get-tuple-element.9.refs_0_, f32[320,256]{1,0:T(8,128)} %get-tuple-element.10.refs_1_, f32[320,256]{1,0:T(8,128)} %get-tuple-element.11.refs_2_), custom_call_target="tpu_custom_call" | custom-call | tf_op jit(solution)/shard_map/pallas_call | solution.py:751

commit v6 on v5

--- a/solution.py
+++ b/solution.py
@@ -188,7 +188,7 @@
                     ]
             return carry
 
-        lax.fori_loop(0, rows_d // 32, body, 0)
+        lax.fori_loop(0, rows_d // 32, body, 0, unroll=True)
 
     def to_narrow(src, dst, half):
         def body(i, carry):
@@ -203,7 +203,7 @@
                 dst[half, pl.ds(i * 32 + h * 16, 16)] = moved[:, h * LANES:(h + 1) * LANES].reshape(16, tiles, LANES)
             return carry
 
-        lax.fori_loop(0, rows_d // 32, body, 0)
+        lax.fori_loop(0, rows_d // 32, body, 0, unroll=True)
 
     def row_at(c, p):
         return c * rows_b + p * CAP
@@ -496,9 +496,16 @@
         attn_sent[q] = copies.start(attn_ref.at[at, 1 - core], a_mate.at[at], mate)
     reached(0)
     reach(1)
+    arrive(*w_pair)
+    in_big, out_big, in_last, out_last = {}, {}, {}, {}
+    in_first = gather_first(in_x, X_RING)
+    in_big[0] = gather_first(in_y(x), Y_RING)
+    out_big[0] = gather_first(out_x(y), X_RING)
+    reached(1)
+    reach(2)
     row_i = lax.broadcasted_iota(jnp.int32, (256, 256), 0)
     col_i = lax.broadcasted_iota(jnp.int32, (256, 256), 1)
-    perm[...] = jnp.where(col_i == (row_i % 16) * 16 + row_i // 16, 1.0, 0.0).astype(BF16)
+    perm[...] = jnp.where(col_i == ((row_i & 15) << 4) + (row_i >> 4), 1.0, 0.0).astype(BF16)
 
     ids_row = ids_ref[...].astype(F32)
     eye_t = lax.broadcasted_iota(jnp.int32, (n_tok, n_tok), 0)
@@ -516,17 +523,12 @@
         axis=1, keepdims=True,
     )
 
-    reached(1)
-    reach(2)
-    arrive(*w_pair)
-    in_first = gather_first(in_x, X_RING)
-    in_big, out_big, in_last, out_last = {}, {}, {}, {}
-    out_big[0] = gather_first(out_x(y), X_RING)
+    attn_ring = attn_begin(attn_sent)
+    out_first = gather_first(out_y, Y_RING)
     pack(tok_ref[...], pk_t)
     x3[core, pl.ds(row_at(block, place), CAP)] = pk_t[pl.ds(block * CAP, CAP)]
     reached(2)
     t_state = z_begin(pk_t, x3)
-    attn_ring = attn_begin(attn_sent)
     @pl.when(at_first)
     def _():
         zr[...] = jnp.zeros_like(zr)
@@ -540,29 +542,27 @@
     slots[BLOCKS * CAP:] = jnp.zeros((slots.shape[0] - BLOCKS * CAP, tiles, LANES), BF16)
 
     z_line(t_state, 1)
+    scatter_middle(attn_ring, lambda i: a_sum.at[i], n_tok, a_r1, a_m3, a_r3, Y_RING)
     z_chain(t_state, 0, 1)
-    scatter_middle(attn_ring, lambda i: a_sum.at[i], n_tok, a_r1, a_m3, a_r3, Y_RING)
-    in_big[0] = gather_first(in_y(x), Y_RING)
-    out_first = gather_first(out_y, Y_RING)
-    z_chain(t_state, 2, 3)
-    z_line(t_state, 2)
     in_next = gather_next(in_first, in_x, X_RING)
     for q in (1, 3):
         in_big[q] = gather_first(in_y((x + q) % NX), Y_RING)
-    z_chain(t_state, 4, 5)
+    z_chain(t_state, 2, 3)
+    z_line(t_state, 2)
+    z_chain(t_state, 4)
     first, second = scatter_end(attn_ring, lambda i: a_sum.at[i], n_tok, a_r2, a_r3, Y_RING)
     summed = jnp.concatenate([first, second], axis=0)
     pack((gate_col * summed).astype(BF16), pk_g)
     g3[core, pl.ds(row_at(block, place), CAP)] = pk_g[pl.ds(block * CAP, CAP)]
     g_state = z_begin(pk_g, g3)
+    z_chain(t_state, 5, 6)
     z_line(t_state, 3)
-    z_chain(t_state, 6, 7)
     arrive(*in_next)
     in_big[2] = gather_first(in_y((x + 2) % NX), Y_RING)
     out_next = gather_next(out_first, out_y, Y_RING)
     for q in (1, 3):
         out_big[q] = gather_first(out_x((y + q) % NY), X_RING)
-    z_chain(t_state, 8)
+    z_chain(t_state, 7, 8)
     t_share = [z_share(t_state, j) for j in range(4)]
     z_line(g_state, 1)
     z_chain(g_state, 0, 1)

time: 121 us -> 119 us (0.983)
  Pallas kernels: 120 us -> 118 us
    pallas_call x1, Pallas kernels: 118 us -> 116 us  [shards(): pl.pallas_call(functools.partial(kernel, (width, hidden)), out_shape=(jax...]
where the time goes in v6:
time: 119 us
  Pallas kernels  118 us (99%)
    pallas_call x1, Pallas kernels, shards(): pl.pallas_call(functools.partial(kernel, (width, hidden)), out_shape=(jax...  116 us

profile of v6, /device:TPU:1, one launch (start us, length us, event | category | flops | bytes accessed | tf_op | source)
XLA Modules:
  0.0 118.7 jit_solution(1244397705035555963)
XLA Ops:
  0.6 116.0 %shard_map.85 = (bf16[64,2048]{1,0:T(8,128)(2,1)}, f32[320,256]{1,0:T(8,128)}, f32[320,256]{1,0:T(8,128)}) custom-call(bf16[64,2048]{1,0:T(8,128)(2,1)} %tok_ref.1, bf16[4,2,64,2048]{3,2,1,0:T(8,128)(2,1)} %bitcast.7, s32[1,64]{1,0:T(1,128)} %bitcast.10, f32[1,64]{1,0:T(1,128)} %bitcast.11, f32[320,256]{1,0:T(8,128)} %bitcast.8, f32[320,256]{1,0:T(8,128)} %bitcast.9), custom_call_target="tpu_custom_call" | custom-call | tf_op jit(solution)/shard_map/pallas_call | solution.py:729
  116.6 2.1 %shard_map.86 = (bf16[64,2048]{1,0:T(8,128)(2,1)}, f32[320,256]{1,0:T(8,128)}, f32[320,256]{1,0:T(8,128)}) custom-call(bf16[64,2048]{1,0:T(8,128)(2,1)} %get-tuple-element.9.refs_0_, f32[320,256]{1,0:T(8,128)} %get-tuple-element.10.refs_1_, f32[320,256]{1,0:T(8,128)} %get-tuple-element.11.refs_2_), custom_call_target="tpu_custom_call" | custom-call | tf_op jit(solution)/shard_map/pallas_call | solution.py:751

commit v7 on v6

--- a/solution.py
+++ b/solution.py
@@ -239,16 +239,25 @@
         to_down = copies.start(blk(above).at[high], blk(above).at[high], lower)
         return [to_up, to_down]
 
-    def scatter_first(blk, count, buf1, buf2, ring):
+    def scatter_far(blk, count, buf1, ring):
         pos, upper, lower = ring
         low, high = halves(count)
-        far, above, below = (pos + 2) % 4, (pos + 1) % 4, (pos + 3) % 4
+        far = (pos + 2) % 4
         return {
             "u1": copies.start(blk(far).at[low], buf1.at[0], upper),
             "d1": copies.start(blk(far).at[high], buf1.at[1], lower),
-            "u2": copies.start(blk(above).at[high], buf2.at[0], upper),
-            "d2": copies.start(blk(below).at[low], buf2.at[1], lower),
         }
+
+    def scatter_near(sent, blk, count, buf2, ring):
+        pos, upper, lower = ring
+        low, high = halves(count)
+        sent["u2"] = copies.start(blk((pos + 1) % 4).at[high], buf2.at[0], upper)
+        sent["d2"] = copies.start(blk((pos + 3) % 4).at[low], buf2.at[1], lower)
+
+    def scatter_first(blk, count, buf1, buf2, ring):
+        sent = scatter_far(blk, count, buf1, ring)
+        scatter_near(sent, blk, count, buf2, ring)
+        return sent
 
     def scatter_middle(sent, blk, count, buf1, mid, buf3, ring):
         pos, upper, lower = ring
@@ -593,28 +602,33 @@
     forward((x + 1) % NX)
     forward((x + 3) % NX)
     to_wide(g3, g2, core)
+    arrive(*in_last[2])
+    forward((x + 2) % NX)
     arrive(*g_share)
     to_wide(g3, g2, 1 - core)
-    out_grads(x)
-    arrive(*out_last[0])
-    hidden_grads(y, True)
-    for q in (1, 3):
-        out_grads((x + q) % NX)
+    def out_block(i):
+        return d_out.at[i]
+
+    def in_block(i):
+        return d_in.at[i]
+
+    out_grads((x + 2) % NX)
+    out_ring = scatter_far(out_block, NY, o_r1, X_RING)
+    for q in range(4):
         arrive(*out_last[q])
-        hidden_grads((y + q) % NY, False)
-    arrive(*in_last[2])
-    forward((x + 2) % NX)
-    out_grads((x + 2) % NX)
-    out_ring = scatter_first(lambda i: d_out.at[i], NY, o_r1, o_r2, X_RING)
-    arrive(*out_last[2])
-    hidden_grads((y + 2) % NY, False)
+        hidden_grads((y + q) % NY, q == 0)
     for i in range(NX):
         grad = (grad_sum[i] * pre_slope[i]).astype(BF16)
         pg[i] = grad
         pg_t[i] = grad.T
-    for q in (2, 1, 3):
-        in_grads((y + q) % NY)
-    in_ring = scatter_first(lambda i: d_in.at[i], NX, i_r1, i_r2, Y_RING)
+    in_grads((y + 2) % NY)
+    in_ring = scatter_far(in_block, NX, i_r1, Y_RING)
+    out_grads((x + 1) % NX)
+    out_grads((x + 3) % NX)
+    scatter_near(out_ring, out_block, NY, o_r2, X_RING)
+    in_grads((y + 1) % NY)
+    in_grads((y + 3) % NY)
+    scatter_near(in_ring, in_block, NX, i_r2, Y_RING)
 
     back = {}
     for part_i in range(2):
@@ -632,29 +646,32 @@
         if part_i == 0:
             for j in order:
                 back[j] = back_share(j)
-            scatter_middle(out_ring, lambda i: d_out.at[i], NY, o_r1, o_m3, o_r3, X_RING)
+    scatter_middle(out_ring, out_block, NY, o_r1, o_m3, o_r3, X_RING)
     for j in order:
         back_sum(back[j], j)
     ends = {}
     back_chain(ends, 0)
+    scatter_middle(in_ring, in_block, NX, i_r1, i_m3, i_r3, Y_RING)
     back_own()
-    back_chain(ends, 1, 2)
+    back_chain(ends, 1)
+    out_grads(x)
     in_grads(y)
-    back_chain(ends, 3, 4)
-    scatter_middle(in_ring, lambda i: d_in.at[i], NX, i_r1, i_m3, i_r3, Y_RING)
-    back_chain(ends, 5, 6, 7, 8)
-    back_own_end()
-
-    first, second = scatter_end(out_ring, lambda i: d_out.at[i], NY, o_r2, o_r3, X_RING)
+    back_chain(ends, 2, 3)
+    first, second = scatter_end(out_ring, out_block, NY, o_r2, o_r3, X_RING)
     o_sum[0:2] = first.astype(BF16)
     o_sum[2:4] = second.astype(BF16)
     out_small = scatter_first(lambda i: o_sum.at[i], share, os_r1, os_r2, Y_RING)
-    first, second = scatter_end(in_ring, lambda i: d_in.at[i], NX, i_r2, i_r3, Y_RING)
+    back_chain(ends, 4, 5)
+    first, second = scatter_end(in_ring, in_block, NX, i_r2, i_r3, Y_RING)
     i_sum[0:2] = first.astype(BF16)
     i_sum[2:4] = second.astype(BF16)
     in_small = scatter_first(lambda i: i_sum.at[i], share, is_r1, is_r2, X_RING)
+    back_chain(ends, 6)
     scatter_middle(out_small, lambda i: o_sum.at[i], share, os_r1, os_m3, os_r3, Y_RING)
+    back_chain(ends, 7)
     scatter_middle(in_small, lambda i: i_sum.at[i], share, is_r1, is_m3, is_r3, X_RING)
+    back_chain(ends, 8)
+    back_own_end()
     pair = []
     for t, sent, sums, buf2, buf3, ring in (
         (1, out_small, o_sum, os_r2, os_r3, Y_RING), (0, in_small, i_sum, is_r2, is_r3, X_RING),

time: 119 us -> 115 us (0.966)
  the two profiles are of different devices: /device:TPU:1 before, /device:TPU:32 now
where the time goes in v7:
time: 115 us
  Pallas kernels  114 us (99%)
    pallas_call x1, Pallas kernels, shards(): pl.pallas_call(functools.partial(kernel, (width, hidden)), out_shape=(jax...  112 us

profile of v7, /device:TPU:32, one launch (start us, length us, event | category | flops | bytes accessed | tf_op | source)
XLA Modules:
  0.0 115.0 jit_solution(18304627843182185225)
XLA Ops:
  0.6 112.3 %shard_map.85 = (bf16[64,2048]{1,0:T(8,128)(2,1)}, f32[320,256]{1,0:T(8,128)}, f32[320,256]{1,0:T(8,128)}) custom-call(bf16[64,2048]{1,0:T(8,128)(2,1)} %tok_ref.1, bf16[4,2,64,2048]{3,2,1,0:T(8,128)(2,1)} %bitcast.7, s32[1,64]{1,0:T(1,128)} %bitcast.10, f32[1,64]{1,0:T(1,128)} %bitcast.11, f32[320,256]{1,0:T(8,128)} %bitcast.8, f32[320,256]{1,0:T(8,128)} %bitcast.9), custom_call_target="tpu_custom_call" | custom-call | tf_op jit(solution)/shard_map/pallas_call | solution.py:746
  112.9 2.1 %shard_map.86 = (bf16[64,2048]{1,0:T(8,128)(2,1)}, f32[320,256]{1,0:T(8,128)}, f32[320,256]{1,0:T(8,128)}) custom-call(bf16[64,2048]{1,0:T(8,128)(2,1)} %get-tuple-element.9.refs_0_, f32[320,256]{1,0:T(8,128)} %get-tuple-element.10.refs_1_, f32[320,256]{1,0:T(8,128)} %get-tuple-element.11.refs_2_), custom_call_target="tpu_custom_call" | custom-call | tf_op jit(solution)/shard_map/pallas_call | solution.py:768

commit v8 on v7

--- a/solution.py
+++ b/solution.py
@@ -589,16 +589,16 @@
     in_last[3] = gather_next(in_big[3], in_y((x + 3) % NX), Y_RING)
     z_chain(g_state, 5)
     z_line(g_state, 3)
-    arrive(*in_last[0])
-    forward(x)
     z_chain(g_state, 6, 7)
     out_last[1] = gather_next(out_big[1], out_x((y + 1) % NY), X_RING)
     out_last[3] = gather_next(out_big[3], out_x((y + 3) % NY), X_RING)
-    arrive(*in_last[1], *in_last[3])
+    arrive(*in_last[0])
+    forward(x)
     z_chain(g_state, 8)
     g_share = [z_share(g_state, j) for j in range(4)]
     in_last[2] = gather_next(in_big[2], in_y((x + 2) % NX), Y_RING)
     out_last[2] = gather_next(out_big[2], out_x((y + 2) % NY), X_RING)
+    arrive(*in_last[1], *in_last[3])
     forward((x + 1) % NX)
     forward((x + 3) % NX)
     to_wide(g3, g2, core)

time: 115 us -> 115 us (level)
  no operation moved by 1% of the time
where the time goes in v8:
time: 115 us
  Pallas kernels  114 us (99%)
    pallas_call x1, Pallas kernels, shards(): pl.pallas_call(functools.partial(kernel, (width, hidden)), out_shape=(jax...  112 us

profile of v8, /device:TPU:32, one launch (start us, length us, event | category | flops | bytes accessed | tf_op | source)
XLA Modules:
  0.0 115.1 jit_solution(1402933678629070130)
XLA Ops:
  0.6 112.3 %shard_map.85 = (bf16[64,2048]{1,0:T(8,128)(2,1)}, f32[320,256]{1,0:T(8,128)}, f32[320,256]{1,0:T(8,128)}) custom-call(bf16[64,2048]{1,0:T(8,128)(2,1)} %tok_ref.1, bf16[4,2,64,2048]{3,2,1,0:T(8,128)(2,1)} %bitcast.7, s32[1,64]{1,0:T(1,128)} %bitcast.10, f32[1,64]{1,0:T(1,128)} %bitcast.11, f32[320,256]{1,0:T(8,128)} %bitcast.8, f32[320,256]{1,0:T(8,128)} %bitcast.9), custom_call_target="tpu_custom_call" | custom-call | tf_op jit(solution)/shard_map/pallas_call | solution.py:746
  113.0 2.1 %shard_map.86 = (bf16[64,2048]{1,0:T(8,128)(2,1)}, f32[320,256]{1,0:T(8,128)}, f32[320,256]{1,0:T(8,128)}) custom-call(bf16[64,2048]{1,0:T(8,128)(2,1)} %get-tuple-element.9.refs_0_, f32[320,256]{1,0:T(8,128)} %get-tuple-element.10.refs_1_, f32[320,256]{1,0:T(8,128)} %get-tuple-element.11.refs_2_), custom_call_target="tpu_custom_call" | custom-call | tf_op jit(solution)/shard_map/pallas_call | solution.py:768
